TPU v7x, 512 devices: a whole 4x4x16 slice. The times are simulated.
512 devices in a mesh: expert: 128 (over z, y, core), tensor: 4 (over x).
Axes of the slice: x: 4, y: 4, z: 16, core: 2. Of those that a mesh axis runs over, the one named last changes fastest.
Arguments:
- tokens: bfloat16 [4096, 1536], P('expert')
- attn_gain: bfloat16 [1536], replicated, may hold values from 0.099609375 to 1.8984375
- query_weight: bfloat16 [1536, 1536], P(None, 'tensor'), may hold values from -0.15625 to 0.15625
- key_value_weight: bfloat16 [4, 1536, 128], P('tensor'), may hold values from -0.15625 to 0.15625
- paired_cache: bfloat16 [128, 4, 768, 128], P('expert', 'tensor')
- prompt_length: int32 [128, 3], P('expert'), may hold values from 1 to 256, 640 in all within a row
- group_index: int32 [4096], P('expert'), may hold values from 0 to 2
- offsets: int32 [4096], P('expert'), may hold values from 0 to 127
- sink_logit: float32 [12], P('tensor'), may hold values from -2 to 4
- out_weight: bfloat16 [1536, 1536], P('tensor'), may hold values from -0.15625 to 0.15625
- mixer_gain: bfloat16 [1536], replicated, may hold values from 0.099609375 to 1.8984375
- routes: int32 [4096, 4], P('expert'), may hold values from 0 to 31, all different within a row; in each aligned block of 8 rows (0 to 7, 8 to 15, ...) at most 2 rows name the same one
- route_weight: float32 [4096, 4], P('expert'), may hold values from 0.05 to 1
- copy_slot: int32 [128], replicated, may hold values from 0 to 127, as said below
- gate_weight: bfloat16 [128, 1536, 768], P('expert', None, 'tensor'), as said below
- up_weight: bfloat16 [128, 1536, 768], P('expert', None, 'tensor'), as said below
- down_weight: bfloat16 [128, 768, 1536], P('expert', 'tensor'), as said below
- final_gain: bfloat16 [1536], P('tensor'), may hold values from 0.099609375 to 1.8984375
Outputs:
- normed: bfloat16 [4096, 1536], P('expert', 'tensor')
Inputs may be any that keep to these rules, and one draw needn't show every extreme that they name: `routes`: in each aligned block of 8 rows no expert is named by more than 2 rows, and in some block one is named by exactly 2. `copy_slot`: a permutation: every slot appears once; slot s lies on expert-axis index s // 1 as its local copy s % 1. `prompt_length`: on every expert-axis index one prompt fills all 256 slots. `gate_weight`: all 4 replicas of an expert hold equal weights. `up_weight`: all 4 replicas of an expert hold equal weights. `down_weight`: all 4 replicas of an expert hold equal weights.
All inputs are finite; a program needn't handle non-finite values.
Results may differ from a plain program's by a relative error of at most 0.013.
Values may be sent and summed in bfloat16 or wider, within the bound.
A program may use at most 64 MiB of HBM per device.

v0:
```python
import jax
import jax.numpy as jnp
from jax import lax
from jax.sharding import PartitionSpec as P

EXPERTS = 32
TOP = 4
PROMPT_CAP = 256
WINDOW = 192


EPSILON = 1e-06


def from_partner(block, axis, apart):
    count = lax.axis_size(axis)
    route = []
    for low in range(count):
        high = low | 1 << apart
        if high != low and high < count:
            route += [(low, high), (high, low)]
    return lax.ppermute(block, axis, route)


def rms_scale(values, gain_row):
    mean_square = jnp.mean(values * values, axis=-1, keepdims=True)
    return values * lax.rsqrt(mean_square + EPSILON) * gain_row.astype(jnp.float32)


def rotate(values, position):
    half_dim = values.shape[-1] // 2
    frequency = 10000.0 ** (-jnp.arange(half_dim, dtype=jnp.float32) / half_dim)
    angles = position.astype(jnp.float32)[:, None] * frequency[None, :]
    if values.ndim == 3:
        angles = angles[:, None, :]
    cosine_part = jnp.cos(angles)
    sine_part = jnp.sin(angles)
    front_half = values[..., :half_dim]
    back_half = values[..., half_dim:]
    return jnp.concatenate(
        [
            front_half * cosine_part - back_half * sine_part,
            front_half * sine_part + back_half * cosine_part,
        ],
        axis=-1,
    )


def slot_places(routes, copy_slot, replicas):
    row_count = routes.shape[0]
    flat_routes = routes.reshape(-1)
    slot_count = flat_routes.shape[0]
    block_of = jnp.arange(slot_count, dtype=jnp.int32) // TOP // (row_count // replicas)
    onehot = (flat_routes[:, None] == jnp.arange(EXPERTS, dtype=jnp.int32)[None, :]).astype(
        jnp.int32
    )
    grouped = onehot.reshape(replicas, slot_count // replicas, EXPERTS)
    earlier = jnp.cumsum(grouped, axis=1) - grouped
    slot_rank = jnp.sum(earlier * grouped, axis=-1).reshape(slot_count)
    holder = copy_slot[flat_routes * replicas + block_of]
    return (holder, slot_rank)


def on_device(
    tokens,
    attn_gain,
    query_weight,
    key_value_weight,
    paired_cache,
    prompt_length,
    group_index,
    offsets,
    sink_logit,
    out_weight,
    mixer_gain,
    routes,
    route_weight,
    copy_slot,
    gate_weight,
    up_weight,
    down_weight,
    final_gain,
):
    lanes = lax.axis_size("tensor")
    member = lax.axis_index("tensor")
    peers = lax.axis_size("expert")
    tok_rows, width = tokens.shape
    head_dim = key_value_weight.shape[2]
    local_heads = query_weight.shape[1] // head_dim
    score_scale = 1.0 / head_dim**0.5
    rows_f32 = tokens.astype(jnp.float32)
    normed_in = rms_scale(rows_f32, attn_gain).astype(jnp.bfloat16)
    lengths = prompt_length[0]
    prompt_slots = jnp.arange(lengths.shape[0], dtype=jnp.int32)
    row_length = jnp.sum(
        jnp.where(group_index[:, None] == prompt_slots[None, :], lengths[None, :], 0), axis=1
    )
    position = row_length + offsets
    queries = jnp.dot(normed_in, query_weight, preferred_element_type=jnp.float32).reshape(
        tok_rows, local_heads, head_dim
    )
    queries = rotate(queries, position).astype(jnp.bfloat16)
    projected = jnp.dot(normed_in, key_value_weight[0], preferred_element_type=jnp.float32)
    marks_key = member % 2 == 0
    own_projection = jnp.where(marks_key, rotate(projected, position), projected).astype(
        jnp.bfloat16
    )
    own_cache = paired_cache[0, 0]
    partner, partner_cache = from_partner((own_projection, own_cache), "tensor", 0)
    new_keys = jnp.where(marks_key, own_projection, partner)
    new_values = jnp.where(marks_key, partner, own_projection)
    cache_keys = jnp.where(marks_key, own_cache, partner_cache)
    cache_values = jnp.where(marks_key, partner_cache, own_cache)
    scores = (
        jnp.einsum("thd,cd->thc", queries, cache_keys, preferred_element_type=jnp.float32)
        * score_scale
    )
    self_score = (
        jnp.sum(queries.astype(jnp.float32) * new_keys.astype(jnp.float32)[:, None, :], axis=-1)
        * score_scale
    )
    slot_index = jnp.arange(cache_keys.shape[0], dtype=jnp.int32)
    slot_group = slot_index // PROMPT_CAP
    slot_pos = slot_index % PROMPT_CAP
    visible = (
        (slot_group[None, :] == group_index[:, None])
        & (slot_pos[None, :] < row_length[:, None])
        & (slot_pos[None, :] > position[:, None] - WINDOW)
    )
    visible = visible[:, None, :]
    masked = jnp.where(visible, scores, -jnp.inf)
    ceiling = jnp.maximum(jnp.maximum(jnp.max(masked, axis=-1), self_score), sink_logit[None, :])
    weights = jnp.where(visible, jnp.exp(scores - ceiling[..., None]), 0.0)
    own_weight = jnp.exp(self_score - ceiling)
    denominator = jnp.sum(weights, axis=-1) + own_weight + jnp.exp(sink_logit[None, :] - ceiling)
    probabilities = (weights / denominator[..., None]).astype(jnp.bfloat16)
    own_prob = (own_weight / denominator).astype(jnp.bfloat16)
    context = jnp.einsum(
        "thc,cd->thd", probabilities, cache_values, preferred_element_type=jnp.float32
    )
    context = (
        context
        + own_prob.astype(jnp.float32)[..., None] * new_values.astype(jnp.float32)[:, None, :]
    )
    context = context.astype(jnp.bfloat16).reshape(tok_rows, local_heads * head_dim)
    attended = jnp.dot(context, out_weight, preferred_element_type=jnp.float32)
    part_width = width // lanes
    feature_start = member * part_width
    copies = copy_slot.shape[0]
    hosted = gate_weight.shape[0]
    replicas = copies // EXPERTS
    capacity = 2 * tok_rows * TOP // (replicas * EXPERTS)
    holders, slot_ranks = slot_places(routes, copy_slot, replicas)
    places = holders * capacity + slot_ranks
    slot_rows = jnp.arange(tok_rows * TOP, dtype=jnp.int32) // TOP
    recv_rows = peers * capacity
    summed = lax.psum(attended.astype(jnp.bfloat16), "tensor").astype(jnp.float32)
    residual_full = (rows_f32 + summed).astype(jnp.bfloat16)
    residual = lax.dynamic_slice_in_dim(residual_full, feature_start, part_width, 1)
    mixed_in = rms_scale(residual_full.astype(jnp.float32), mixer_gain).astype(jnp.bfloat16)
    features = mixed_in.shape[1]
    outbox = (
        jnp.zeros((copies * capacity, features), jnp.bfloat16).at[places].set(mixed_in[slot_rows])
    )
    received = lax.all_to_all(
        outbox.reshape(peers, hosted * capacity, features),
        "expert",
        split_axis=0,
        concat_axis=0,
        tiled=True,
    )
    to_features = received.shape[2]
    received = (
        received.reshape(peers, hosted, capacity, to_features)
        .transpose(1, 0, 2, 3)
        .reshape(hosted, recv_rows, to_features)
    )
    gate_val = jnp.einsum("hrd,hdf->hrf", received, gate_weight, preferred_element_type=jnp.float32)
    up_val = jnp.einsum("hrd,hdf->hrf", received, up_weight, preferred_element_type=jnp.float32)
    hidden = (jnp.maximum(gate_val, 0.0) * up_val).astype(jnp.bfloat16)
    partial_sums = jnp.einsum(
        "hrf,hfd->hrd", hidden, down_weight, preferred_element_type=jnp.float32
    )
    shares = lax.psum_scatter(
        partial_sums.astype(jnp.bfloat16), "tensor", scatter_dimension=2, tiled=True
    )
    outgoing = (
        shares.reshape(hosted, peers, capacity, part_width)
        .transpose(1, 0, 2, 3)
        .reshape(peers, hosted * capacity, part_width)
    )
    returned = lax.all_to_all(outgoing, "expert", split_axis=0, concat_axis=0, tiled=True).reshape(
        copies * capacity, part_width
    )
    per_slot = returned[places].astype(jnp.float32).reshape(tok_rows, TOP, part_width)
    mixture = jnp.sum(route_weight[:, :, None] * per_slot, axis=1)
    combined = residual.astype(jnp.float32) + mixture
    totals = lax.psum(jnp.sum(combined * combined, axis=1), "tensor")
    return (
        combined
        * lax.rsqrt(totals[:, None] / width + EPSILON)
        * final_gain.astype(jnp.float32)[None, :]
    ).astype(jnp.bfloat16)


def solution(mesh):
    in_specs = (
        P("expert", None),
        P(),
        P(None, "tensor"),
        P("tensor", None, None),
        P("expert", "tensor", None, None),
        P("expert", None),
        P("expert"),
        P("expert"),
        P("tensor"),
        P("tensor", None),
        P(),
        P("expert", None),
        P("expert", None),
        P(),
        P("expert", None, "tensor"),
        P("expert", None, "tensor"),
        P("expert", "tensor", None),
        P("tensor"),
    )
    out_specs = P("expert", "tensor")
    return jax.shard_map(
        on_device, mesh=mesh, in_specs=in_specs, out_specs=out_specs, check_vma=False
    )
```

profile of v0, /device:TPU:1, one launch (start us, length us, event | category | flops | bytes accessed | tf_op | source)
XLA Modules:
  0.0 232.1 jit_solution(2419648842832018313)
XLA Ops:
  6.6 0.8 convert_element_type.95
  7.3 1.0 fusion.17
  8.4 0.8 select_reduce_fusion.2
  9.1 0.7 broadcast_add_fusion
  9.8 1.3 fusion.8
  11.1 0.1 multiply_subtract_fusion
  11.3 3.9 %collective-permute-start.1 = (bf16[32,128]{1,0:T(8,128)(2,1)S(1)}, bf16[32,128]{1,0:T(8,128)(2,1)S(1)}, u32[]{:S(2)}, u32[]{:S(2)}) collective-permute-start(bf16[32,128]{1,0:T(8,128)(2,1)S(1)} %fusion.36), channel_id=1, source_target_pairs={{0,1},{1,0},{2,3},{3,2},{4,5},{5,4},{6,7},{7,6},{8,9},{9,8},{10,11... | collective-permute-start | bytes 24584 | tf_op jit(solution)/shard_map/ppermute | solution.py:22
  15.3 1.9 collective-permute-start
  17.2 0.1 multiply_cosine_fusion
  17.3 0.8 copy.41
  18.1 0.7 broadcast_multiply_fusion
  18.8 1.7 fusion.34
  20.5 0.1 fusion.53
  20.7 0.1 fusion.30
  20.9 0.2 select_reduce_fusion.1
  21.3 0.1 mul.246
  21.5 1.2 gather_fusion
  22.7 0.1 compare_and_fusion
  22.9 0.2 multiply_reduce_fusion.2
  23.1 0.3 select_reduce_fusion
  23.5 0.2 fusion.13
  23.8 0.3 fusion.3
  24.1 1.0 convolution_convert_fusion.1
  25.1 60.0 %all-reduce.2.cloned.1.call-done = bf16[32,1536]{1,0:T(8,128)(2,1)} async-done(((bf16[32,1536]{1,0:T(8,128)(2,1)}), bf16[32,1536]{1,0:T(8,128)(2,1)}) %all-reduce.2.cloned.1.call-update) | async-done | bytes 98320 | tf_op jit(solution)/shard_map/psum | solution.py:157
  85.2 1.0 fusion.14
  86.2 0.6 copy-done.3
  86.8 0.1 fusion.16
  86.9 2.7 %scatter_custom_fusion = bf16[256,1536]{1,0:T(8,128)(2,1)S(1)} fusion(s32[128]{0:T(128)S(1)} %fusion.47, bf16[32,1536]{1,0:T(8,128)(2,1)S(1)} %fusion.16, s32[1024]{0:T(1024)S(1)} %pad_clamp_fusion.1, bf16[]{:T(256)} %constant.111.clone.1), kind=kCustom, calls=%fused_computation.21 | custom fusion | bytes 786434 | tf_op jit(solution)/shard_map/scatter | solution.py:163
  89.7 0.3 reshape.443
  90.0 60.1 %all_to_all.10 = bf16[128,2,1536]{2,1,0:T(2,128)(2,1)S(1)} all-to-all(bf16[128,2,1536]{2,1,0:T(2,128)(2,1)S(1)} %reshape.443), channel_id=1, replica_groups=mesh['expert'=128,'tensor'=4] {'expert'}, dimensions={0} | all-to-all | bytes 1572864 | tf_op jit(solution)/shard_map/all_to_all | solution.py:165
  150.1 0.3 reshape.444
  150.4 0.8 copy-done.5
  151.2 0.4 convolution_maximum_fusion
  151.6 2.4 %fusion = bf16[1,256,1536]{2,1,0:T(8,128)(2,1)S(1)} fusion(f32[256,192]{0,1:T(8,128)S(1)} %convolution_maximum_fusion, bf16[256,1536]{1,0:T(8,128)(2,1)S(1)} %reshape.444, bf16[1,192,1536]{2,1,0:T(8,128)(2,1)} %param.34, bf16[1,1536,192]{1,2,0:T(8,128)(2,1)} %param.33), kind=kOutput, calls=%fused_computation.5 | convolution fusion | flops 302481408 | bytes 2949120 | tf_op jit(solution)/shard_map/hrf,hfd->hrd/dot_general | solution.py:181
  154.0 1.2 copy.42
  155.2 1.0 copy.57
  156.3 21.3 %reduce-scatter.4.cloned.1.call-done = bf16[384,256]{1,0:T(8,128)(2,1)} async-done(((bf16[1536,256]{1,0:T(8,128)(2,1)}), bf16[384,256]{1,0:T(8,128)(2,1)}) %reduce-scatter.4.cloned.1.call-update) | async-done | bytes 196624
  177.5 1.1 reshape_bitcast_fusion
  178.7 0.6 copy.43
  179.3 0.7 reshape_transpose_reshape.4
  180.0 19.0 %all-to-all-start.1 = ((bf16[128,2,384]{2,1,0:T(2,128)(2,1)}), bf16[128,2,384]{2,1,0:T(2,128)(2,1)S(1)}, u32[]{:S(2)}, u32[]{:S(2)}) async-start(bf16[128,2,384]{2,1,0:T(2,128)(2,1)} %reshape_transpose_reshape.4), calls=%async_computation.1 | async-start | bytes 393216 | tf_op jit(solution)/shard_map/all_to_all | solution.py:192
  199.1 0.1 copy.39
  199.2 17.9 %all-to-all-done.1 = bf16[128,2,384]{2,1,0:T(2,128)(2,1)S(1)} async-done(((bf16[128,2,384]{2,1,0:T(2,128)(2,1)}), bf16[128,2,384]{2,1,0:T(2,128)(2,1)S(1)}, u32[]{:S(2)}, u32[]{:S(2)}) %all-to-all-start.1) | async-done | bytes 196640 | tf_op jit(solution)/shard_map/all_to_all | solution.py:192
  217.2 0.9 gather_fusion.1
  218.1 0.2 multiply_reduce_fusion
  218.3 0.1 multiply_reduce_fusion.1
  218.4 6.1 %psum.15 = f32[32]{0:T(128)S(1)} all-reduce(f32[32]{0:T(128)S(1)} %multiply_reduce_fusion.1), channel_id=1, replica_groups=mesh['expert'=128,'tensor'=4] {'tensor'}, use_global_device_ids=true, to_apply=%region_13.14 | all-reduce | flops 32 | bytes 256 | tf_op jit(solution)/shard_map/psum | solution.py:198
  224.5 0.7 multiply_convert_fusion
  (53 shorter events, 1.0 us)
Async XLA Ops:
  6.5 17.5 %copy-start = (bf16[384,1536]{1,0:T(8,128)(2,1)S(1)}, bf16[384,1536]{1,0:T(8,128)(2,1)}, u32[]{:S(2)}) copy-start(bf16[384,1536]{1,0:T(8,128)(2,1)} %param.27) | copy-start | bytes 3538948
  6.5 78.6 %all-reduce.2.cloned.1.call-start = ((), (), s32[]{:S(2)}) async-start(), calls=%async_computation.3 | async-start | bytes 196608 | tf_op jit(solution)/shard_map/psum | solution.py:157
  11.1 10.4 %copy-start.1 = (s32[128]{0:T(128)S(1)}, s32[128]{0:T(128)}, u32[]{:S(2)}) copy-start(s32[128]{0:T(128)} %param.31) | copy-start | bytes 1540
  11.3 11.6 %collective-permute-start.1 = (bf16[32,128]{1,0:T(8,128)(2,1)S(1)}, bf16[32,128]{1,0:T(8,128)(2,1)S(1)}, u32[]{:S(2)}, u32[]{:S(2)}) collective-permute-start(bf16[32,128]{1,0:T(8,128)(2,1)S(1)} %fusion.36), channel_id=1, source_target_pairs={{0,1},{1,0},{2,3},{3,2},{4,5},{5,4},{6,7},{7,6},{8,9},{9,8},{10,11... | collective-permute-start | bytes 24584 | tf_op jit(solution)/shard_map/ppermute | solution.py:22
  15.3 7.8 %collective-permute-start = (bf16[768,128]{1,0:T(8,128)(2,1)}, bf16[768,128]{1,0:T(8,128)(2,1)S(1)}, u32[]{:S(2)}, u32[]{:S(2)}) collective-permute-start(bf16[768,128]{1,0:T(8,128)(2,1)} %bitcast.62), channel_id=1, source_target_pairs={{0,1},{1,0},{2,3},{3,2},{4,5},{5,4},{6,7},{7,6},{8,9},{9,8},{10,11... | collective-permute-start | bytes 589832 | tf_op jit(solution)/shard_map/ppermute | solution.py:22
  18.8 3.9 %copy-start.11 = (s32[32]{0:T(128)S(1)}, s32[32]{0:T(128)}, u32[]{:S(2)}) copy-start(s32[32]{0:T(128)} %param.24) | copy-start | bytes 388
  18.8 4.1 %copy-start.7 = (bf16[1536]{0:T(1024)(128)(2,1)S(1)}, bf16[1536]{0:T(1024)(128)(2,1)}, u32[]{:S(2)}) copy-start(bf16[1536]{0:T(1024)(128)(2,1)} %param.28) | copy-start | bytes 9220
  18.8 4.3 %copy-start.6 = (bf16[1,1,768,128]{3,2,1,0:T(8,128)(2,1)S(1)}, bf16[1,1,768,128]{3,2,1,0:T(8,128)(2,1)}, u32[]{:S(2)}) copy-start(bf16[1,1,768,128]{3,2,1,0:T(8,128)(2,1)} %param.22) | copy-start | bytes 589828
  20.5 2.9 %copy-start.9 = (f32[3]{0:T(128)S(1)}, f32[3]{0:T(128)}, u32[]{:S(2)}) copy-start(f32[3]{0:T(128)} %param.26) | copy-start | bytes 40
  23.8 61.4 %copy-start.2 = (bf16[32,1536]{1,0:T(8,128)(2,1)S(1)}, bf16[32,1536]{1,0:T(8,128)(2,1)}, u32[]{:S(2)}) copy-start(bf16[32,1536]{1,0:T(8,128)(2,1)} %param.18) | copy-start | bytes 294916
  25.1 152.5 %reduce-scatter.4.cloned.1.call-start = ((), (), s32[]{:S(2)}) async-start(), calls=%async_computation.4 | async-start | bytes 983040
  86.2 0.6 copy-start.3
  150.1 1.1 copy-start.5
  156.2 42.8 %copy-start.8 = (f32[32,4]{0,1:T(4,128)S(1)}, f32[32,4]{0,1:T(4,128)}, u32[]{:S(2)}) copy-start(f32[32,4]{0,1:T(4,128)} %param.30) | copy-start | bytes 1540
  156.3 42.9 %copy-start.10 = (bf16[384]{0:T(512)(128)(2,1)S(1)}, bf16[384]{0:T(512)(128)(2,1)}, u32[]{:S(2)}) copy-start(bf16[384]{0:T(512)(128)(2,1)} %param.35) | copy-start | bytes 2308
  180.0 38.3 %copy-start.4 = (bf16[32,1536]{1,0:T(8,128)(2,1)S(1)}, bf16[32,1536]{1,0:T(8,128)(2,1)}, u32[]{:S(2)}) copy-start(bf16[32,1536]{1,0:T(8,128)(2,1)} %copy-done.3) | copy-start | bytes 294916
  180.0 37.1 %all-to-all-start.1 = ((bf16[128,2,384]{2,1,0:T(2,128)(2,1)}), bf16[128,2,384]{2,1,0:T(2,128)(2,1)S(1)}, u32[]{:S(2)}, u32[]{:S(2)}) async-start(bf16[128,2,384]{2,1,0:T(2,128)(2,1)} %reshape_transpose_reshape.4), calls=%async_computation.1 | async-start | bytes 393216 | tf_op jit(solution)/shard_map/all_to_all | solution.py:192
Sparse Core Ops, SparseCore 0:
  25.2 59.9 all-reduce.1
  156.4 21.1 reduce-scatter.3
where the time goes:
time: 235 us; the launch traced here: 232 us
  waiting for transfers between devices  99.3 us (42%)
  blocking collectives  66.2 us (28%)
  starting transfers between devices  24.9 us (11%)
  between operations  13.8 us (6%)
  local copies, waits for them, and re-layouts  13 us (6%)
  other arithmetic  7.5 us (3%)
  matrix products  7.34 us (3%)
    all_to_all x1, blocking collectives, on_device(): lax.all_to_all(outbox.reshape(peers, hosted * capacity, features), 'exper...  60.1 us
    psum x1, waiting for transfers between devices, on_device(): lax.psum(attended.astype(jnp.bfloat16), 'tensor').astype(jnp.float32)  60 us
    unnamed x3, waiting for transfers between devices  21.3 us
    all_to_all x1, starting transfers between devices, on_device(): lax.all_to_all(outgoing, 'expert', split_axis=0, concat_axis=0, tiled=True)  19 us
    all_to_all x1, waiting for transfers between devices, on_device(): lax.all_to_all(outgoing, 'expert', split_axis=0, concat_axis=0, tiled=True)  17.9 us
    unnamed x30, local copies, waits for them, and re-layouts  6.24 us
    psum x1, blocking collectives, on_device(): totals = lax.psum(jnp.sum(combined * combined, axis=1), 'tensor')  6.11 us
    ppermute x2, starting transfers between devices, from_partner(): return lax.ppermute(block, axis, route)  5.85 us
  transfers between devices with their start and end apart: 5, of which 3 were waited for; matrix products, arithmetic and copies ran while one was open for 3% of the time, Pallas kernels for 0%

commit v1 on v0

--- a/solution.py
+++ b/solution.py
@@ -1,6 +1,8 @@
 import jax
 import jax.numpy as jnp
 from jax import lax
+from jax.experimental import pallas as pl
+from jax.experimental.pallas import tpu as pltpu
 from jax.sharding import PartitionSpec as P
 
 EXPERTS = 32
@@ -46,19 +48,426 @@
     )
 
 
-def slot_places(routes, copy_slot, replicas):
-    row_count = routes.shape[0]
-    flat_routes = routes.reshape(-1)
-    slot_count = flat_routes.shape[0]
-    block_of = jnp.arange(slot_count, dtype=jnp.int32) // TOP // (row_count // replicas)
-    onehot = (flat_routes[:, None] == jnp.arange(EXPERTS, dtype=jnp.int32)[None, :]).astype(
-        jnp.int32
-    )
-    grouped = onehot.reshape(replicas, slot_count // replicas, EXPERTS)
-    earlier = jnp.cumsum(grouped, axis=1) - grouped
-    slot_rank = jnp.sum(earlier * grouped, axis=-1).reshape(slot_count)
-    holder = copy_slot[flat_routes * replicas + block_of]
-    return (holder, slot_rank)
+def slot_places(routes, copy_slot):
+    rows = routes.shape[0]
+    copies = copy_slot.shape[0]
+    replicas = copies // EXPERTS
+    block = jnp.arange(rows, dtype=jnp.int32) // (rows // replicas)
+    row = jnp.arange(rows, dtype=jnp.int32)
+    earlier = (block[:, None] == block[None, :]) & (row[None, :] < row[:, None])
+    same = routes[:, :, None, None] == routes[None, None, :, :]
+    rank = jnp.sum((same & earlier[:, None, :, None]).astype(jnp.int32), axis=(2, 3))
+    wanted = routes * replicas + block[:, None]
+    picks = wanted[:, :, None] == jnp.arange(copies, dtype=jnp.int32)
+    holder = jnp.sum(jnp.where(picks, copy_slot, 0), axis=-1)
+    return (holder % PLANE) * (2 * RING) + (holder // PLANE) * 2 + rank
+
+
+RING = 16
+PLANE = 8
+LANES = 4
+PART = 384
+MESH = pl.DeviceIdType.MESH
+
+
+def far_first(t):
+    half = (t + 1) // 2
+    return RING // 2 + half * (1 - 2 * (t % 2))
+
+
+def remote(src, dst, send, recv, expert, tensor):
+    return pltpu.make_async_remote_copy(
+        src_ref=src,
+        dst_ref=dst,
+        send_sem=send,
+        recv_sem=recv,
+        device_id=(expert, tensor),
+        device_id_type=MESH,
+    )
+
+
+def dot(a, b):
+    return jnp.dot(a, b, preferred_element_type=jnp.float32)
+
+
+def moe_kernel(
+    context_ref,
+    out_weight_ref,
+    tokens_ref,
+    mixer_ref,
+    places_ref,
+    places_t_ref,
+    route_weight_ref,
+    gate_ref,
+    up_ref,
+    down_ref,
+    final_ref,
+    out_ref,
+    att,
+    att_in,
+    sq,
+    sq_in,
+    plane_out,
+    plane_in,
+    ring_out,
+    box,
+    partial,
+    partial_in,
+    sums,
+    sums_in,
+    back_out,
+    back_in,
+    s_att,
+    r_att,
+    s_sq,
+    r_sq,
+    s_plane,
+    r_plane,
+    s_ring,
+    r_ring,
+    s_box,
+    r_box,
+    s_part,
+    r_part,
+    s_sum,
+    r_sum,
+    s_back,
+    r_back,
+):
+    me = lax.axis_index("expert")
+    x = lax.axis_index("tensor")
+    z = me // PLANE
+    yc = me % PLANE
+    rows = tokens_ref.shape[0]
+    width = LANES * PART
+
+    barrier = pltpu.get_barrier_semaphore()
+
+    def greet(expert, tensor):
+        pl.semaphore_signal(barrier, inc=1, device_id=(expert, tensor), device_id_type=MESH)
+
+    @pl.loop(1, RING)
+    def _(d):
+        greet((z + d) % RING * PLANE + yc, x)
+
+    @pl.loop(1, PLANE)
+    def _(d):
+        greet(z * PLANE + (yc + d) % PLANE, x)
+
+    @pl.loop(1, LANES)
+    def _(d):
+        greet(me, (x + d) % LANES)
+
+    context = context_ref[...]
+    for j in range(LANES):
+        att[j] = dot(context, out_weight_ref[:, j * PART : (j + 1) * PART]).astype(jnp.bfloat16)
+    pl.semaphore_wait(barrier, RING + PLANE + LANES - 3)
+
+    def att_copy(d):
+        to = (x + d) % LANES
+        return remote(att.at[to], att_in.at[d - 1], s_att.at[d - 1], r_att.at[d - 1], me, to)
+
+    for d in range(1, LANES):
+        att_copy(d).start()
+    mine = pl.ds(pl.multiple_of(x * PART, 128), PART)
+    summed = att[x].astype(jnp.float32)
+    for d in range(1, LANES):
+        att_copy(d).wait_recv()
+        summed = summed + att_in[d - 1].astype(jnp.float32)
+    summed = summed.astype(jnp.bfloat16).astype(jnp.float32)
+    residual = (tokens_ref[:, mine].astype(jnp.float32) + summed).astype(jnp.bfloat16)
+    residual = residual.astype(jnp.float32)
+
+    def whole_square(values, which):
+        own = jnp.sum(values * values, axis=1, keepdims=True)
+        sq[which] = jnp.broadcast_to(own, (rows, 128))
+
+        def copy(d):
+            to = (x + d) % LANES
+            return remote(
+                sq.at[which],
+                sq_in.at[which, d - 1],
+                s_sq.at[which, d - 1],
+                r_sq.at[which, d - 1],
+                me,
+                to,
+            )
+
+        for d in range(1, LANES):
+            copy(d).start()
+        total = own
+        for d in range(1, LANES):
+            copy(d).wait_recv()
+            total = total + sq_in[which, d - 1][:, :1]
+        for d in range(1, LANES):
+            copy(d).wait_send()
+        return total
+
+    total = whole_square(residual, 0)
+    gain = mixer_ref[:, mine].astype(jnp.float32)
+    mixed = (residual * lax.rsqrt(total / width + EPSILON) * gain).astype(jnp.bfloat16)
+
+    slots = 2 * RING * PLANE
+    place_row = lax.broadcasted_iota(jnp.int32, (slots, rows), 0)
+    taken = jnp.zeros((slots, rows), jnp.float32)
+    for k in range(TOP):
+        taken = taken + (places_t_ref[k : k + 1, :] == place_row).astype(jnp.float32)
+    outbox = dot(taken.astype(jnp.bfloat16), mixed).astype(jnp.bfloat16)
+    plane_out[...] = outbox.reshape(PLANE, 2 * RING, PART)
+
+    def plane_copy(d):
+        to = (yc + d) % PLANE
+        return remote(
+            plane_out.at[to], plane_in.at[yc], s_plane.at[d], r_plane.at[d], z * PLANE + to, x
+        )
+
+    def plane_arrival(d):
+        return remote(
+            plane_out.at[yc],
+            plane_in.at[(yc + PLANE - d) % PLANE],
+            s_plane.at[d],
+            r_plane.at[d],
+            me,
+            (x + 1) % LANES,
+        )
+
+    @pl.loop(1, PLANE)
+    def _(d):
+        plane_copy(d).start()
+
+    plane_in[yc] = plane_out[yc]
+
+    @pl.loop(1, PLANE)
+    def _(d):
+        plane_arrival(d).wait_recv()
+
+    to_row = lax.broadcasted_iota(jnp.int32, (slots, slots), 0)
+    from_row = lax.broadcasted_iota(jnp.int32, (slots, slots), 1)
+    by_ring = ((to_row >> 1) & (PLANE - 1)) * (2 * RING) + (to_row >> 4) * 2 + (to_row & 1)
+    by_ring = (by_ring == from_row).astype(jnp.float32).astype(jnp.bfloat16)
+    by_plane = ((to_row >> 1) & (RING - 1)) * (2 * PLANE) + (to_row >> 5) * 2 + (to_row & 1)
+    by_plane = (by_plane == from_row).astype(jnp.float32).astype(jnp.bfloat16)
+    ordered = dot(by_ring, plane_in[...].reshape(slots, PART)).astype(jnp.bfloat16)
+    ring_out[...] = ordered.reshape(RING, 2 * PLANE, PART)
+
+    def ring_copy(d):
+        to = (z + d) % RING
+        return remote(
+            ring_out.at[to], box.at[x, z], s_ring.at[d], r_ring.at[d], to * PLANE + yc, x
+        )
+
+    def ring_arrival(d):
+        return remote(
+            ring_out.at[z],
+            box.at[x, (z + RING - d) % RING],
+            s_ring.at[d],
+            r_ring.at[d],
+            me,
+            (x + 1) % LANES,
+        )
+
+    def box_copy(d, j):
+        at = (z + RING - d) % RING
+        return remote(
+            box.at[x, at],
+            box.at[x, at],
+            s_box.at[d, j - 1],
+            r_box.at[d, j - 1],
+            me,
+            (x + j) % LANES,
+        )
+
+    def box_arrival(d, j):
+        at = (z + RING - d) % RING
+        return remote(
+            box.at[x, at],
+            box.at[(x + LANES - j) % LANES, at],
+            s_box.at[d, j - 1],
+            r_box.at[d, j - 1],
+            me,
+            (x + j) % LANES,
+        )
+
+    @pl.loop(0, RING - 1)
+    def _(t):
+        ring_copy(far_first(t)).start()
+
+    box[x, z] = ring_out[z]
+    for j in range(1, LANES):
+        box_copy(0, j).start()
+
+    @pl.loop(0, RING - 1)
+    def _(t):
+        d = far_first(t)
+        ring_arrival(d).wait_recv()
+        for j in range(1, LANES):
+            box_copy(d, j).start()
+
+    @pl.loop(0, RING)
+    def _(d):
+        for j in range(1, LANES):
+            box_arrival(d, j).wait_recv()
+
+    gate_val = jnp.zeros((slots, gate_ref.shape[1]), jnp.float32)
+    up_val = jnp.zeros((slots, gate_ref.shape[1]), jnp.float32)
+    for j in range(LANES):
+        part = box[j].reshape(slots, PART)
+        gate_val = gate_val + dot(part, gate_ref[j * PART : (j + 1) * PART, :])
+        up_val = up_val + dot(part, up_ref[j * PART : (j + 1) * PART, :])
+    hidden = (jnp.maximum(gate_val, 0.0) * up_val).astype(jnp.bfloat16)
+    for j in range(LANES):
+        product = dot(hidden, down_ref[:, j * PART : (j + 1) * PART]).astype(jnp.bfloat16)
+        partial[j] = product.reshape(RING, 2 * PLANE, PART)
+
+    def part_copy(d, j):
+        at = (z + d) % RING
+        to = (x + j) % LANES
+        return remote(
+            partial.at[to, at],
+            partial_in.at[j - 1, at],
+            s_part.at[d, j - 1],
+            r_part.at[d, j - 1],
+            me,
+            to,
+        )
+
+    def sum_copy(d):
+        to = (z + d) % RING
+        return remote(sums.at[to], sums_in.at[z], s_sum.at[d], r_sum.at[d], to * PLANE + yc, x)
+
+    def sum_arrival(d):
+        return remote(
+            sums.at[z],
+            sums_in.at[(z + RING - d) % RING],
+            s_sum.at[d],
+            r_sum.at[d],
+            me,
+            (x + 1) % LANES,
+        )
+
+    @pl.loop(0, RING)
+    def _(t):
+        for j in range(1, LANES):
+            part_copy(far_first(t), j).start()
+
+    def add_parts(d):
+        at = (z + d) % RING
+        value = partial[x, at].astype(jnp.float32)
+        for j in range(1, LANES):
+            part_copy(d, j).wait_recv()
+            value = value + partial_in[j - 1, at].astype(jnp.float32)
+        return value.astype(jnp.bfloat16)
+
+    @pl.loop(0, RING - 1)
+    def _(t):
+        d = far_first(t)
+        sums[(z + d) % RING] = add_parts(d)
+        sum_copy(d).start()
+
+    sums_in[z] = add_parts(0)
+
+    @pl.loop(1, RING)
+    def _(d):
+        sum_arrival(d).wait_recv()
+
+    ordered = dot(by_plane, sums_in[...].reshape(slots, PART)).astype(jnp.bfloat16)
+    back_out[...] = ordered.reshape(PLANE, 2 * RING, PART)
+
+    def back_copy(d):
+        to = (yc + d) % PLANE
+        return remote(
+            back_out.at[to], back_in.at[yc], s_back.at[d], r_back.at[d], z * PLANE + to, x
+        )
+
+    def back_arrival(d):
+        return remote(
+            back_out.at[yc],
+            back_in.at[(yc + PLANE - d) % PLANE],
+            s_back.at[d],
+            r_back.at[d],
+            me,
+            (x + 1) % LANES,
+        )
+
+    @pl.loop(1, PLANE)
+    def _(d):
+        back_copy(d).start()
+
+    back_in[yc] = back_out[yc]
+    place_col = lax.broadcasted_iota(jnp.int32, (rows, slots), 1)
+    weigh = jnp.zeros((rows, slots), jnp.float32)
+    for k in range(TOP):
+        hit = places_ref[:, k : k + 1] == place_col
+        weigh = weigh + jnp.where(hit, route_weight_ref[:, k : k + 1], 0.0)
+    high = weigh.astype(jnp.bfloat16)
+    low = (weigh - high.astype(jnp.float32)).astype(jnp.bfloat16)
+
+    @pl.loop(1, PLANE)
+    def _(d):
+        back_arrival(d).wait_recv()
+
+    returned = back_in[...].reshape(slots, PART)
+    combined = residual + (dot(high, returned) + dot(low, returned))
+    total = whole_square(combined, 1)
+    final = final_ref[...].astype(jnp.float32)
+    out_ref[...] = (combined * lax.rsqrt(total / width + EPSILON) * final).astype(out_ref.dtype)
+
+    for d in range(1, LANES):
+        att_copy(d).wait_send()
+
+    @pl.loop(1, PLANE)
+    def _(d):
+        plane_copy(d).wait_send()
+        back_copy(d).wait_send()
+
+    @pl.loop(1, RING)
+    def _(d):
+        ring_copy(d).wait_send()
+        sum_copy(d).wait_send()
+
+    @pl.loop(0, RING)
+    def _(d):
+        for j in range(1, LANES):
+            box_copy(d, j).wait_send()
+            part_copy(d, j).wait_send()
+
+
+def moe_call(*operands):
+    rows = operands[2].shape[0]
+    vmem, sem = pltpu.VMEM, pltpu.SemaphoreType.DMA
+    bf16 = jnp.bfloat16
+    by_plane = vmem((PLANE, 2 * RING, PART), bf16)
+    by_ring = vmem((RING, 2 * PLANE, PART), bf16)
+    return pl.pallas_call(
+        moe_kernel,
+        out_shape=jax.ShapeDtypeStruct((rows, PART), bf16),
+        in_specs=[pl.BlockSpec(memory_space=pltpu.VMEM)] * len(operands),
+        out_specs=pl.BlockSpec(memory_space=pltpu.VMEM),
+        scratch_shapes=[
+            vmem((LANES, rows, PART), bf16),
+            vmem((LANES - 1, rows, PART), bf16),
+            vmem((2, rows, 128), jnp.float32),
+            vmem((2, LANES - 1, rows, 128), jnp.float32),
+            by_plane,
+            by_plane,
+            by_ring,
+            vmem((LANES, RING, 2 * PLANE, PART), bf16),
+            vmem((LANES, RING, 2 * PLANE, PART), bf16),
+            vmem((LANES - 1, RING, 2 * PLANE, PART), bf16),
+            by_ring,
+            by_ring,
+            by_plane,
+            by_plane,
+        ]
+        + [sem((LANES - 1,))] * 2
+        + [sem((2, LANES - 1))] * 2
+        + [sem((PLANE,))] * 2
+        + [sem((RING,))] * 2
+        + [sem((RING, LANES - 1))] * 4
+        + [sem((RING,))] * 2
+        + [sem((PLANE,))] * 2,
+        compiler_params=pltpu.CompilerParams(collective_id=0, has_side_effects=True),
+    )(*operands)
 
 
 def on_device(
@@ -143,64 +552,20 @@
         + own_prob.astype(jnp.float32)[..., None] * new_values.astype(jnp.float32)[:, None, :]
     )
     context = context.astype(jnp.bfloat16).reshape(tok_rows, local_heads * head_dim)
-    attended = jnp.dot(context, out_weight, preferred_element_type=jnp.float32)
-    part_width = width // lanes
-    feature_start = member * part_width
-    copies = copy_slot.shape[0]
-    hosted = gate_weight.shape[0]
-    replicas = copies // EXPERTS
-    capacity = 2 * tok_rows * TOP // (replicas * EXPERTS)
-    holders, slot_ranks = slot_places(routes, copy_slot, replicas)
-    places = holders * capacity + slot_ranks
-    slot_rows = jnp.arange(tok_rows * TOP, dtype=jnp.int32) // TOP
-    recv_rows = peers * capacity
-    summed = lax.psum(attended.astype(jnp.bfloat16), "tensor").astype(jnp.float32)
-    residual_full = (rows_f32 + summed).astype(jnp.bfloat16)
-    residual = lax.dynamic_slice_in_dim(residual_full, feature_start, part_width, 1)
-    mixed_in = rms_scale(residual_full.astype(jnp.float32), mixer_gain).astype(jnp.bfloat16)
-    features = mixed_in.shape[1]
-    outbox = (
-        jnp.zeros((copies * capacity, features), jnp.bfloat16).at[places].set(mixed_in[slot_rows])
-    )
-    received = lax.all_to_all(
-        outbox.reshape(peers, hosted * capacity, features),
-        "expert",
-        split_axis=0,
-        concat_axis=0,
-        tiled=True,
-    )
-    to_features = received.shape[2]
-    received = (
-        received.reshape(peers, hosted, capacity, to_features)
-        .transpose(1, 0, 2, 3)
-        .reshape(hosted, recv_rows, to_features)
-    )
-    gate_val = jnp.einsum("hrd,hdf->hrf", received, gate_weight, preferred_element_type=jnp.float32)
-    up_val = jnp.einsum("hrd,hdf->hrf", received, up_weight, preferred_element_type=jnp.float32)
-    hidden = (jnp.maximum(gate_val, 0.0) * up_val).astype(jnp.bfloat16)
-    partial_sums = jnp.einsum(
-        "hrf,hfd->hrd", hidden, down_weight, preferred_element_type=jnp.float32
-    )
-    shares = lax.psum_scatter(
-        partial_sums.astype(jnp.bfloat16), "tensor", scatter_dimension=2, tiled=True
-    )
-    outgoing = (
-        shares.reshape(hosted, peers, capacity, part_width)
-        .transpose(1, 0, 2, 3)
-        .reshape(peers, hosted * capacity, part_width)
-    )
-    returned = lax.all_to_all(outgoing, "expert", split_axis=0, concat_axis=0, tiled=True).reshape(
-        copies * capacity, part_width
-    )
-    per_slot = returned[places].astype(jnp.float32).reshape(tok_rows, TOP, part_width)
-    mixture = jnp.sum(route_weight[:, :, None] * per_slot, axis=1)
-    combined = residual.astype(jnp.float32) + mixture
-    totals = lax.psum(jnp.sum(combined * combined, axis=1), "tensor")
-    return (
-        combined
-        * lax.rsqrt(totals[:, None] / width + EPSILON)
-        * final_gain.astype(jnp.float32)[None, :]
-    ).astype(jnp.bfloat16)
+    places = slot_places(routes, copy_slot)
+    return moe_call(
+        context,
+        out_weight,
+        tokens,
+        mixer_gain.reshape(1, width),
+        places,
+        places.T,
+        route_weight,
+        gate_weight[0],
+        up_weight[0],
+        down_weight[0],
+        final_gain.reshape(1, -1),
+    )
 
 
 def solution(mesh):

time: 235 us -> 100 us (0.43); the launches traced: 232 us -> 99.6 us
  waiting for transfers between devices: 99.3 us -> 0.01 us
  Pallas kernels: 0 us -> 75.8 us
  blocking collectives: 66.2 us -> 0 us
  starting transfers between devices: 24.9 us -> 5.85 us
  between operations: 13.8 us -> 0.19 us
  local copies, waits for them, and re-layouts: 13 us -> 6.51 us
  matrix products: 7.34 us -> 3.14 us
    pallas_call x0 -> x1, Pallas kernels: none -> 75.8 us  [moe_call(): pl.pallas_call(moe_kernel, out_shape=jax.ShapeDtypeStruct((rows, PART), b...]
    all_to_all x1 -> x0, blocking collectives: 60.1 us -> none  [on_device(): lax.all_to_all(outbox.reshape(peers, hosted * capacity, features), 'exper...]
    psum x1 -> x0, waiting for transfers between devices: 60 us -> none  [on_device(): lax.psum(attended.astype(jnp.bfloat16), 'tensor').astype(jnp.float32)]
    unnamed x3 -> x0, waiting for transfers between devices: 21.3 us -> none
    all_to_all x1 -> x0, starting transfers between devices: 19 us -> none  [on_device(): lax.all_to_all(outgoing, 'expert', split_axis=0, concat_axis=0, tiled=True)]
    all_to_all x1 -> x0, waiting for transfers between devices: 17.9 us -> none  [on_device(): lax.all_to_all(outgoing, 'expert', split_axis=0, concat_axis=0, tiled=True)]
    psum x1 -> x0, blocking collectives: 6.11 us -> none  [on_device(): totals = lax.psum(jnp.sum(combined * combined, axis=1), 'tensor')]
    dot_general x3 -> x0, matrix products: 3.75 us -> none  [the longest x1 2.39 us: on_device(): jnp.einsum('hrf,hfd->hrd', hidden, down_weight, preferred_element_type=jn...]
  transfers between devices with their start and end apart: 5 -> 2, of which waited for: 3 -> 0; matrix products, arithmetic and copies ran while one was open for 3% -> 10% of each run, Pallas kernels for 0% -> 0%
where the time goes in v1:
time: 100 us; the launch traced here: 99.6 us
  Pallas kernels  75.8 us (76%)
  other arithmetic  8.09 us (8%)
  local copies, waits for them, and re-layouts  6.51 us (7%)
  starting transfers between devices  5.85 us (6%)
  matrix products  3.14 us (3%)
    pallas_call x1, Pallas kernels, moe_call(): pl.pallas_call(moe_kernel, out_shape=jax.ShapeDtypeStruct((rows, PART), b...  75.8 us
    ppermute x2, starting transfers between devices, from_partner(): return lax.ppermute(block, axis, route)  5.85 us
    unnamed x22, local copies, waits for them, and re-layouts  4.41 us
  transfers between devices with their start and end apart: 2, of which 0 were waited for; matrix products, arithmetic and copies ran while one was open for 10% of the time, Pallas kernels for 0%

profile of v1, /device:TPU:1, one launch (start us, length us, event | category | flops | bytes accessed | tf_op | source)
XLA Modules:
  0.0 99.6 jit_solution(2266875041786157376)
XLA Ops:
  0.0 0.0 copy-start
  0.0 1.1 %fusion.5 = f32[32]{0:T(128)S(1)} fusion(bf16[32,1536]{1,0:T(8,128)(2,1)} %tokens_ref.1), kind=kLoop, calls=%fused_computation.13 | loop fusion | flops 147424 | bytes 98432 | tf_op jit(solution)/shard_map/reduce_sum | solution.py:28
  1.1 0.7 convert_element_type.50
  1.8 0.8 select_reduce_fusion.2
  2.6 0.7 broadcast_add_fusion
  3.3 1.3 %fusion.2 = f32[32,128]{1,0:T(8,128)S(1)} fusion(bf16[1,1536,128]{2,1,0:T(8,128)(2,1)} %param.21, bf16[32,1536]{1,0:T(8,128)(2,1)} %tokens_ref.1, f32[1536]{0:T(1024)S(1)} %convert_element_type.50, f32[32]{0:T(128)S(1)} %add_rsqrt_fusion), kind=kOutput, calls=%fused_computation.4 | convolution fusion | flops 12779520 | bytes 514176 | tf_op jit(solution)/shard_map/dot_general | solution.py:512
  4.6 0.0 copy-start.7
  4.6 0.0 copy-start.4
  4.6 0.0 copy-start.5
  4.6 0.0 copy-start.1
  4.6 0.1 multiply_subtract_fusion
  4.8 0.1 fusion.24
  4.8 3.9 %collective-permute-start.1 = (bf16[32,128]{1,0:T(8,128)(2,1)S(1)}, bf16[32,128]{1,0:T(8,128)(2,1)S(1)}, u32[]{:S(2)}, u32[]{:S(2)}) collective-permute-start(bf16[32,128]{1,0:T(8,128)(2,1)S(1)} %fusion.24), channel_id=1, source_target_pairs={{0,1},{1,0},{2,3},{3,2},{4,5},{5,4},{6,7},{7,6},{8,9},{9,8},{10,11... | collective-permute-start | bytes 24584 | tf_op jit(solution)/shard_map/ppermute | solution.py:24
  8.8 1.9 %collective-permute-start = (bf16[768,128]{1,0:T(8,128)(2,1)}, bf16[768,128]{1,0:T(8,128)(2,1)S(1)}, u32[]{:S(2)}, u32[]{:S(2)}) collective-permute-start(bf16[768,128]{1,0:T(8,128)(2,1)} %bitcast.53), channel_id=1, source_target_pairs={{0,1},{1,0},{2,3},{3,2},{4,5},{5,4},{6,7},{7,6},{8,9},{9,8},{10,11... | collective-permute-start | bytes 589832 | tf_op jit(solution)/shard_map/ppermute | solution.py:24
  10.7 0.1 multiply_cosine_fusion
  10.9 0.1 fusion.29
  10.9 0.7 multiply_add_fusion.1
  11.6 1.0 convert_reduce_fusion
  12.6 0.9 select_reduce_fusion.1
  13.5 0.1 copy.53
  13.6 0.1 copy.58
  13.7 0.0 copy-done
  13.7 1.2 %fusion.18 = f32[32,384]{1,0:T(8,128)S(1)} fusion(bf16[1536,384]{1,0:T(8,128)(2,1)S(1)} %copy-done, bf16[32,1536]{1,0:T(8,128)(2,1)} %tokens_ref.1, f32[1536]{0:T(1024)S(1)} %convert_element_type.50, f32[32]{0:T(128)S(1)} %add_rsqrt_fusion), kind=kOutput, calls=%fused_computation.38 | convolution fusion | flops 37945344 | bytes 1333376 | tf_op jit(solution)/shard_map/dot_general | solution.py:508
  14.9 0.0 copy-start.2
  15.0 0.1 fusion.49
  15.1 0.6 fusion.22.places_ref
  15.7 0.0 copy-done.8
  15.7 0.1 compare_and_fusion
  15.8 0.6 fusion.39.places_t_ref
  16.4 0.0 copy-done.7
  16.4 0.6 reshape.316.final_ref
  17.0 0.0 copy-done.4
  17.0 0.6 reshape.315.mixer_ref
  17.6 0.0 copy-done.5
  17.6 0.7 copy.61.route_weight_ref
  18.3 1.1 %copy.59 = bf16[1,1536,192]{2,1,0:T(8,128)(2,1)} copy(bf16[1,1536,192]{1,2,0:T(8,128)(2,1)S(1)} %copy-done.1) | data formatting | bytes 1179648 | tf_op args[14]
  19.5 1.2 %copy.60 = bf16[1,1536,192]{2,1,0:T(8,128)(2,1)} copy(bf16[1,1536,192]{1,2,0:T(8,128)(2,1)S(1)} %copy-done.2) | data formatting | bytes 1179648 | tf_op args[15]
  20.6 0.0 collective-permute-done.1
  20.6 0.2 multiply_reduce_fusion
  20.8 0.0 collective-permute-done
  20.8 0.3 select_reduce_fusion
  21.2 0.1 maximum_maximum_fusion
  21.2 0.2 fusion.4
  21.5 0.1 fusion.44
  21.5 0.3 fusion.1
  21.8 0.6 copy.70
  22.4 75.8 %shard_map.172 = bf16[32,384]{1,0:T(8,128)(2,1)} custom-call(bf16[32,384]{1,0:T(8,128)(2,1)} %bitcast.54, bf16[384,1536]{1,0:T(8,128)(2,1)} %out_weight_ref.1, bf16[32,1536]{1,0:T(8,128)(2,1)} %tokens_ref.1, bf16[1,1536]{1,0:T(2,128)(2,1)} %reshape.315.mixer_ref, s32[32,4]{1,0:T(8,128)} %fusion.22.places_ref, s32[4,32]{1,0:T(4,128)} %fusion.39.places_t_ref, ...), custom_call_target="tpu_custom_call" | custom-call | tf_op jit(solution)/shard_map/pallas_call | solution.py:441
  98.3 1.3 %copy.72 = bf16[32,384]{1,0:T(8,128)(2,1)} copy(bf16[32,384]{1,0:T(8,128)(2,1)} %shard_map.172) | data formatting | bytes 49152
  (14 shorter events, 0.1 us)
Async XLA Ops:
  0.0 13.7 %copy-start = (bf16[1536,384]{1,0:T(8,128)(2,1)S(1)}, bf16[1536,384]{1,0:T(8,128)(2,1)}, u32[]{:S(2)}) copy-start(bf16[1536,384]{1,0:T(8,128)(2,1)} %param.20) | copy-start | bytes 3538948
  3.3 12.4 %copy-start.8 = (s32[32]{0:T(128)S(1)}, s32[32]{0:T(128)}, u32[]{:S(2)}) copy-start(s32[32]{0:T(128)} %param.24) | copy-start | bytes 388
  4.6 11.9 %copy-start.7 = (bf16[384]{0:T(512)(128)(2,1)S(1)}, bf16[384]{0:T(512)(128)(2,1)}, u32[]{:S(2)}) copy-start(bf16[384]{0:T(512)(128)(2,1)} %param.35) | copy-start | bytes 2308
  4.6 12.4 %copy-start.4 = (bf16[1536]{0:T(1024)(128)(2,1)S(1)}, bf16[1536]{0:T(1024)(128)(2,1)}, u32[]{:S(2)}) copy-start(bf16[1536]{0:T(1024)(128)(2,1)} %param.28) | copy-start | bytes 9220
  4.6 13.0 %copy-start.5 = (f32[32,4]{0,1:T(4,128)S(1)}, f32[32,4]{0,1:T(4,128)}, u32[]{:S(2)}) copy-start(f32[32,4]{0,1:T(4,128)} %param.30) | copy-start | bytes 1540
  4.6 13.7 %copy-start.1 = (bf16[1,1536,192]{1,2,0:T(8,128)(2,1)S(1)}, bf16[1,1536,192]{1,2,0:T(8,128)(2,1)}, u32[]{:S(2)}) copy-start(bf16[1,1536,192]{1,2,0:T(8,128)(2,1)} %param.32) | copy-start | bytes 1769476
  4.8 15.8 %collective-permute-start.1 = (bf16[32,128]{1,0:T(8,128)(2,1)S(1)}, bf16[32,128]{1,0:T(8,128)(2,1)S(1)}, u32[]{:S(2)}, u32[]{:S(2)}) collective-permute-start(bf16[32,128]{1,0:T(8,128)(2,1)S(1)} %fusion.24), channel_id=1, source_target_pairs={{0,1},{1,0},{2,3},{3,2},{4,5},{5,4},{6,7},{7,6},{8,9},{9,8},{10,11... | collective-permute-start | bytes 24584 | tf_op jit(solution)/shard_map/ppermute | solution.py:24
  8.8 12.0 %collective-permute-start = (bf16[768,128]{1,0:T(8,128)(2,1)}, bf16[768,128]{1,0:T(8,128)(2,1)S(1)}, u32[]{:S(2)}, u32[]{:S(2)}) collective-permute-start(bf16[768,128]{1,0:T(8,128)(2,1)} %bitcast.53), channel_id=1, source_target_pairs={{0,1},{1,0},{2,3},{3,2},{4,5},{5,4},{6,7},{7,6},{8,9},{9,8},{10,11... | collective-permute-start | bytes 589832 | tf_op jit(solution)/shard_map/ppermute | solution.py:24
  14.9 4.6 %copy-start.2 = (bf16[1,1536,192]{1,2,0:T(8,128)(2,1)S(1)}, bf16[1,1536,192]{1,2,0:T(8,128)(2,1)}, u32[]{:S(2)}) copy-start(bf16[1,1536,192]{1,2,0:T(8,128)(2,1)} %param.33) | copy-start | bytes 1769476
  18.3 2.5 %copy-start.3 = (bf16[1,1,768,128]{3,2,1,0:T(8,128)(2,1)S(1)}, bf16[1,1,768,128]{3,2,1,0:T(8,128)(2,1)}, u32[]{:S(2)}) copy-start(bf16[1,1,768,128]{3,2,1,0:T(8,128)(2,1)} %param.22) | copy-start | bytes 589828
  19.5 1.7 %copy-start.6 = (f32[3]{0:T(128)S(1)}, f32[3]{0:T(128)}, u32[]{:S(2)}) copy-start(f32[3]{0:T(128)} %param.26) | copy-start | bytes 40

commit v2 on v1

--- a/solution.py
+++ b/solution.py
@@ -67,6 +67,7 @@
 PLANE = 8
 LANES = 4
 PART = 384
+LAG = 3
 MESH = pl.DeviceIdType.MESH
 
 
@@ -88,6 +89,10 @@
 
 def dot(a, b):
     return jnp.dot(a, b, preferred_element_type=jnp.float32)
+
+
+def dot_t(a, b):
+    return lax.dot_general(a, b, (((1,), (1,)), ((), ())), preferred_element_type=jnp.float32)
 
 
 def moe_kernel(
@@ -113,6 +118,7 @@
     box,
     partial,
     partial_in,
+    joint,
     sums,
     sums_in,
     back_out,
@@ -288,47 +294,84 @@
             (x + j) % LANES,
         )
 
+    def relay_copy(d):
+        at = (z + RING - d) % RING
+        turn = d % 2
+        lane = (x + LANES - 1 + 2 * turn) % LANES
+        return remote(
+            box.at[lane, at],
+            box.at[lane, at],
+            s_box.at[d, 1],
+            r_box.at[d, 1],
+            me,
+            (x + 1 + 2 * turn) % LANES,
+        )
+
+    def relay(d):
+        box_arrival(d, 1 + 2 * (d % 2)).wait_recv()
+        relay_copy(d).start()
+
     @pl.loop(0, RING - 1)
     def _(t):
         ring_copy(far_first(t)).start()
 
     box[x, z] = ring_out[z]
-    for j in range(1, LANES):
-        box_copy(0, j).start()
-
-    @pl.loop(0, RING - 1)
+    box_copy(0, 1).start()
+    box_copy(0, 3).start()
+
+    def pass_on(d):
+        ring_arrival(d).wait_recv()
+        box_copy(d, 1).start()
+        box_copy(d, 3).start()
+
+    pass_on(far_first(0))
+    relay(0)
+
+    @pl.loop(1, RING - 1)
     def _(t):
-        d = far_first(t)
-        ring_arrival(d).wait_recv()
-        for j in range(1, LANES):
-            box_copy(d, j).start()
+        pass_on(far_first(t))
+        relay(far_first(t - 1))
+
+    relay(far_first(RING - 2))
 
     @pl.loop(0, RING)
     def _(d):
-        for j in range(1, LANES):
-            box_arrival(d, j).wait_recv()
-
-    gate_val = jnp.zeros((slots, gate_ref.shape[1]), jnp.float32)
-    up_val = jnp.zeros((slots, gate_ref.shape[1]), jnp.float32)
+        box_arrival(d, 3 - 2 * (d % 2)).wait_recv()
+        box_arrival(d, 2).wait_recv()
+
+    gate_val = jnp.zeros((slots, gate_ref.shape[0]), jnp.float32)
+    up_val = jnp.zeros((slots, gate_ref.shape[0]), jnp.float32)
     for j in range(LANES):
         part = box[j].reshape(slots, PART)
-        gate_val = gate_val + dot(part, gate_ref[j * PART : (j + 1) * PART, :])
-        up_val = up_val + dot(part, up_ref[j * PART : (j + 1) * PART, :])
+        gate_val = gate_val + dot_t(part, gate_ref[:, j * PART : (j + 1) * PART])
+        up_val = up_val + dot_t(part, up_ref[:, j * PART : (j + 1) * PART])
     hidden = (jnp.maximum(gate_val, 0.0) * up_val).astype(jnp.bfloat16)
     for j in range(LANES):
         product = dot(hidden, down_ref[:, j * PART : (j + 1) * PART]).astype(jnp.bfloat16)
         partial[j] = product.reshape(RING, 2 * PLANE, PART)
 
-    def part_copy(d, j):
+    def towards(d):
+        return (x + 1 + 2 * (d % 2)) % LANES
+
+    def away(d):
+        return (x + LANES - 1 + 2 * (d % 2)) % LANES
+
+    def near_copy(d):
+        at, to = (z + d) % RING, towards(d)
+        return remote(
+            partial.at[to, at], partial_in.at[0, at], s_part.at[d, 0], r_part.at[d, 0], me, to
+        )
+
+    def far_copy(d):
+        at, to = (z + d) % RING, (x + 2) % LANES
+        return remote(
+            partial.at[to, at], partial_in.at[1, at], s_part.at[d, 1], r_part.at[d, 1], me, away(d)
+        )
+
+    def joint_copy(d):
         at = (z + d) % RING
-        to = (x + j) % LANES
-        return remote(
-            partial.at[to, at],
-            partial_in.at[j - 1, at],
-            s_part.at[d, j - 1],
-            r_part.at[d, j - 1],
-            me,
-            to,
+        return remote(
+            joint.at[at], partial_in.at[2, at], s_part.at[d, 2], r_part.at[d, 2], me, away(d)
         )
 
     def sum_copy(d):
@@ -347,19 +390,33 @@
 
     @pl.loop(0, RING)
     def _(t):
-        for j in range(1, LANES):
-            part_copy(far_first(t), j).start()
+        d = far_first(t)
+        far_copy(d).start()
+        near_copy(d).start()
+
+    def join(d):
+        at = (z + d) % RING
+        far_copy(d).wait_recv()
+        value = partial[away(d), at].astype(jnp.float32) + partial_in[1, at].astype(jnp.float32)
+        joint[at] = value.astype(jnp.bfloat16)
+        joint_copy(d).start()
 
     def add_parts(d):
         at = (z + d) % RING
-        value = partial[x, at].astype(jnp.float32)
-        for j in range(1, LANES):
-            part_copy(d, j).wait_recv()
-            value = value + partial_in[j - 1, at].astype(jnp.float32)
-        return value.astype(jnp.bfloat16)
+        near_copy(d).wait_recv()
+        joint_copy(d).wait_recv()
+        value = partial[x, at].astype(jnp.float32) + partial_in[0, at].astype(jnp.float32)
+        return (value + partial_in[2, at].astype(jnp.float32)).astype(jnp.bfloat16)
+
+    for t in range(LAG):
+        join(far_first(t))
 
     @pl.loop(0, RING - 1)
     def _(t):
+        @pl.when(t + LAG < RING)
+        def _():
+            join(far_first(t + LAG))
+
         d = far_first(t)
         sums[(z + d) % RING] = add_parts(d)
         sum_copy(d).start()
@@ -427,9 +484,12 @@
 
     @pl.loop(0, RING)
     def _(d):
-        for j in range(1, LANES):
-            box_copy(d, j).wait_send()
-            part_copy(d, j).wait_send()
+        box_copy(d, 1).wait_send()
+        box_copy(d, 3).wait_send()
+        relay_copy(d).wait_send()
+        near_copy(d).wait_send()
+        far_copy(d).wait_send()
+        joint_copy(d).wait_send()
 
 
 def moe_call(*operands):
@@ -454,6 +514,7 @@
             vmem((LANES, RING, 2 * PLANE, PART), bf16),
             vmem((LANES, RING, 2 * PLANE, PART), bf16),
             vmem((LANES - 1, RING, 2 * PLANE, PART), bf16),
+            by_ring,
             by_ring,
             by_ring,
             by_plane,
@@ -561,8 +622,8 @@
         places,
         places.T,
         route_weight,
-        gate_weight[0],
-        up_weight[0],
+        gate_weight[0].T,
+        up_weight[0].T,
         down_weight[0],
         final_gain.reshape(1, -1),
     )

time: 100 us -> 119 us (1.19)
  Pallas kernels: 75.8 us -> 99.4 us
  local copies, waits for them, and re-layouts: 6.51 us -> 4.19 us
  other arithmetic: 8.09 us -> 6 us
    pallas_call x1, Pallas kernels: 75.8 us -> 99.4 us  [moe_call(): pl.pallas_call(moe_kernel, out_shape=jax.ShapeDtypeStruct((rows, PART), b...]
    unnamed x22 -> x20, local copies, waits for them, and re-layouts: 4.41 us -> 2.08 us
  transfers between devices with their start and end apart: 2 -> 2, of which waited for: 0 -> 0; matrix products, arithmetic and copies ran while one was open for 10% -> 5% of each run, Pallas kernels for 0% -> 0%
where the time goes in v2:
time: 119 us
  Pallas kernels  99.4 us (84%)
  other arithmetic  6 us (5%)
  starting transfers between devices  5.99 us (5%)
  local copies, waits for them, and re-layouts  4.19 us (4%)
  matrix products  3.15 us (3%)
    pallas_call x1, Pallas kernels, moe_call(): pl.pallas_call(moe_kernel, out_shape=jax.ShapeDtypeStruct((rows, PART), b...  99.4 us
    ppermute x2, starting transfers between devices, from_partner(): return lax.ppermute(block, axis, route)  5.99 us
  transfers between devices with their start and end apart: 2, of which 0 were waited for; matrix products, arithmetic and copies ran while one was open for 5% of the time, Pallas kernels for 0%

profile of v2, /device:TPU:1, one launch (start us, length us, event | category | flops | bytes accessed | tf_op | source)
XLA Modules:
  0.0 119.0 jit_solution(8933882028250943568)
XLA Ops:
  0.0 0.0 copy-start
  0.0 0.8 convert_element_type.50
  0.8 1.0 fusion.5
  1.8 0.8 select_reduce_fusion.2
  2.6 0.7 broadcast_add_fusion
  3.3 1.3 %fusion.2 = f32[32,128]{1,0:T(8,128)S(1)} fusion(bf16[1,1536,128]{2,1,0:T(8,128)(2,1)} %param.21, bf16[32,1536]{1,0:T(8,128)(2,1)} %tokens_ref.1, f32[1536]{0:T(1024)S(1)} %convert_element_type.50, f32[32]{0:T(128)S(1)} %add_rsqrt_fusion), kind=kOutput, calls=%fused_computation.4 | convolution fusion | flops 12779520 | bytes 514176 | tf_op jit(solution)/shard_map/dot_general | solution.py:573
  4.6 0.0 copy-start.4
  4.6 0.0 copy-start.3
  4.6 0.0 copy-start.6
  4.6 0.1 multiply_subtract_fusion
  4.8 0.0 copy-start.1
  4.8 0.1 fusion.24
  4.9 4.1 %collective-permute-start.1 = (bf16[32,128]{1,0:T(8,128)(2,1)S(1)}, bf16[32,128]{1,0:T(8,128)(2,1)S(1)}, u32[]{:S(2)}, u32[]{:S(2)}) collective-permute-start(bf16[32,128]{1,0:T(8,128)(2,1)S(1)} %fusion.24), channel_id=1, source_target_pairs={{0,1},{1,0},{2,3},{3,2},{4,5},{5,4},{6,7},{7,6},{8,9},{9,8},{10,11... | collective-permute-start | bytes 24584 | tf_op jit(solution)/shard_map/ppermute | solution.py:24
  8.9 1.9 %collective-permute-start = (bf16[768,128]{1,0:T(8,128)(2,1)}, bf16[768,128]{1,0:T(8,128)(2,1)S(1)}, u32[]{:S(2)}, u32[]{:S(2)}) collective-permute-start(bf16[768,128]{1,0:T(8,128)(2,1)} %bitcast.57), channel_id=1, source_target_pairs={{0,1},{1,0},{2,3},{3,2},{4,5},{5,4},{6,7},{7,6},{8,9},{9,8},{10,11... | collective-permute-start | bytes 589832 | tf_op jit(solution)/shard_map/ppermute | solution.py:24
  10.9 0.1 multiply_cosine_fusion
  11.0 0.0 copy-done
  11.0 0.0 copy-start.5
  11.0 1.2 %fusion.18 = f32[32,384]{1,0:T(8,128)S(1)} fusion(bf16[1536,384]{1,0:T(8,128)(2,1)S(1)} %copy-done, bf16[32,1536]{1,0:T(8,128)(2,1)} %tokens_ref.1, f32[1536]{0:T(1024)S(1)} %convert_element_type.50, f32[32]{0:T(128)S(1)} %add_rsqrt_fusion), kind=kOutput, calls=%fused_computation.38 | convolution fusion | flops 37945344 | bytes 1333376 | tf_op jit(solution)/shard_map/dot_general | solution.py:569
  12.3 0.1 fusion.49
  12.4 0.1 fusion.29
  12.5 0.0 copy-done.2
  12.5 0.2 convert_reduce_fusion
  12.7 0.1 copy.52
  12.8 0.0 copy-done.8
  12.8 0.2 select_reduce_fusion.1
  13.1 0.1 copy.47
  13.1 0.6 fusion.22.places_ref
  13.8 0.0 copy-done.7
  13.8 0.1 compare_and_fusion
  13.9 0.6 fusion.39.places_t_ref
  14.5 0.0 copy-done.4
  14.5 0.7 copy.53.route_weight_ref
  15.2 0.0 copy-done.3
  15.2 0.6 reshape.315.mixer_ref
  15.8 0.0 copy-done.6
  15.8 0.6 reshape.316.final_ref
  16.4 0.0 collective-permute-done.1
  16.4 0.2 multiply_reduce_fusion
  16.6 0.0 collective-permute-done
  16.6 0.0 copy-done.1
  16.6 0.3 select_reduce_fusion
  16.9 0.1 maximum_maximum_fusion
  17.0 0.2 fusion.4
  17.2 0.1 fusion.44
  17.3 0.3 fusion.1
  17.6 0.6 copy.62
  18.2 99.4 %shard_map.172 = bf16[32,384]{1,0:T(8,128)(2,1)} custom-call(bf16[32,384]{1,0:T(8,128)(2,1)} %bitcast.58, bf16[384,1536]{1,0:T(8,128)(2,1)} %out_weight_ref.1, bf16[32,1536]{1,0:T(8,128)(2,1)} %tokens_ref.1, bf16[1,1536]{1,0:T(2,128)(2,1)} %reshape.315.mixer_ref, s32[32,4]{1,0:T(8,128)} %fusion.22.places_ref, s32[4,32]{1,0:T(4,128)} %fusion.39.places_t_ref, ...), custom_call_target="tpu_custom_call" | custom-call | tf_op jit(solution)/shard_map/pallas_call | solution.py:501
  117.6 1.3 %copy.64 = bf16[32,384]{1,0:T(8,128)(2,1)} copy(bf16[32,384]{1,0:T(8,128)(2,1)} %shard_map.172) | data formatting | bytes 49152
  (12 shorter events, 0.1 us)
Async XLA Ops:
  0.0 11.0 %copy-start = (bf16[1536,384]{1,0:T(8,128)(2,1)S(1)}, bf16[1536,384]{1,0:T(8,128)(2,1)}, u32[]{:S(2)}) copy-start(bf16[1536,384]{1,0:T(8,128)(2,1)} %param.20) | copy-start | bytes 3538948
  3.3 9.2 %copy-start.2 = (s32[32,4]{0,1:T(4,128)S(1)}, s32[32,4]{0,1:T(4,128)}, u32[]{:S(2)}) copy-start(s32[32,4]{0,1:T(4,128)} %param.29) | copy-start | bytes 1540
  3.3 9.6 %copy-start.8 = (s32[128]{0:T(128)S(1)}, s32[128]{0:T(128)}, u32[]{:S(2)}) copy-start(s32[128]{0:T(128)} %param.31) | copy-start | bytes 1540
  3.3 10.5 %copy-start.7 = (s32[32]{0:T(128)S(1)}, s32[32]{0:T(128)}, u32[]{:S(2)}) copy-start(s32[32]{0:T(128)} %param.24) | copy-start | bytes 388
  4.6 9.9 %copy-start.4 = (f32[32,4]{0,1:T(4,128)S(1)}, f32[32,4]{0,1:T(4,128)}, u32[]{:S(2)}) copy-start(f32[32,4]{0,1:T(4,128)} %param.30) | copy-start | bytes 1540
  4.6 10.6 %copy-start.3 = (bf16[1536]{0:T(1024)(128)(2,1)S(1)}, bf16[1536]{0:T(1024)(128)(2,1)}, u32[]{:S(2)}) copy-start(bf16[1536]{0:T(1024)(128)(2,1)} %param.28) | copy-start | bytes 9220
  4.6 11.2 %copy-start.6 = (bf16[384]{0:T(512)(128)(2,1)S(1)}, bf16[384]{0:T(512)(128)(2,1)}, u32[]{:S(2)}) copy-start(bf16[384]{0:T(512)(128)(2,1)} %param.35) | copy-start | bytes 2308
  4.8 11.8 %copy-start.1 = (bf16[1,1,768,128]{3,2,1,0:T(8,128)(2,1)S(1)}, bf16[1,1,768,128]{3,2,1,0:T(8,128)(2,1)}, u32[]{:S(2)}) copy-start(bf16[1,1,768,128]{3,2,1,0:T(8,128)(2,1)} %param.22) | copy-start | bytes 589828
  4.9 11.5 %collective-permute-start.1 = (bf16[32,128]{1,0:T(8,128)(2,1)S(1)}, bf16[32,128]{1,0:T(8,128)(2,1)S(1)}, u32[]{:S(2)}, u32[]{:S(2)}) collective-permute-start(bf16[32,128]{1,0:T(8,128)(2,1)S(1)} %fusion.24), channel_id=1, source_target_pairs={{0,1},{1,0},{2,3},{3,2},{4,5},{5,4},{6,7},{7,6},{8,9},{9,8},{10,11... | collective-permute-start | bytes 24584 | tf_op jit(solution)/shard_map/ppermute | solution.py:24
  8.9 7.6 %collective-permute-start = (bf16[768,128]{1,0:T(8,128)(2,1)}, bf16[768,128]{1,0:T(8,128)(2,1)S(1)}, u32[]{:S(2)}, u32[]{:S(2)}) collective-permute-start(bf16[768,128]{1,0:T(8,128)(2,1)} %bitcast.57), channel_id=1, source_target_pairs={{0,1},{1,0},{2,3},{3,2},{4,5},{5,4},{6,7},{7,6},{8,9},{9,8},{10,11... | collective-permute-start | bytes 589832 | tf_op jit(solution)/shard_map/ppermute | solution.py:24
  11.0 5.9 %copy-start.5 = (f32[3]{0:T(128)S(1)}, f32[3]{0:T(128)}, u32[]{:S(2)}) copy-start(f32[3]{0:T(128)} %param.26) | copy-start | bytes 40

commit v3 on v1

--- a/solution.py
+++ b/solution.py
@@ -1,5 +1,6 @@
 import jax
 import jax.numpy as jnp
+import numpy as np
 from jax import lax
 from jax.experimental import pallas as pl
 from jax.experimental.pallas import tpu as pltpu
@@ -14,59 +15,18 @@
 EPSILON = 1e-06
 
 
-def from_partner(block, axis, apart):
-    count = lax.axis_size(axis)
-    route = []
-    for low in range(count):
-        high = low | 1 << apart
-        if high != low and high < count:
-            route += [(low, high), (high, low)]
-    return lax.ppermute(block, axis, route)
-
-
 def rms_scale(values, gain_row):
     mean_square = jnp.mean(values * values, axis=-1, keepdims=True)
     return values * lax.rsqrt(mean_square + EPSILON) * gain_row.astype(jnp.float32)
-
-
-def rotate(values, position):
-    half_dim = values.shape[-1] // 2
-    frequency = 10000.0 ** (-jnp.arange(half_dim, dtype=jnp.float32) / half_dim)
-    angles = position.astype(jnp.float32)[:, None] * frequency[None, :]
-    if values.ndim == 3:
-        angles = angles[:, None, :]
-    cosine_part = jnp.cos(angles)
-    sine_part = jnp.sin(angles)
-    front_half = values[..., :half_dim]
-    back_half = values[..., half_dim:]
-    return jnp.concatenate(
-        [
-            front_half * cosine_part - back_half * sine_part,
-            front_half * sine_part + back_half * cosine_part,
-        ],
-        axis=-1,
-    )
-
-
-def slot_places(routes, copy_slot):
-    rows = routes.shape[0]
-    copies = copy_slot.shape[0]
-    replicas = copies // EXPERTS
-    block = jnp.arange(rows, dtype=jnp.int32) // (rows // replicas)
-    row = jnp.arange(rows, dtype=jnp.int32)
-    earlier = (block[:, None] == block[None, :]) & (row[None, :] < row[:, None])
-    same = routes[:, :, None, None] == routes[None, None, :, :]
-    rank = jnp.sum((same & earlier[:, None, :, None]).astype(jnp.int32), axis=(2, 3))
-    wanted = routes * replicas + block[:, None]
-    picks = wanted[:, :, None] == jnp.arange(copies, dtype=jnp.int32)
-    holder = jnp.sum(jnp.where(picks, copy_slot, 0), axis=-1)
-    return (holder % PLANE) * (2 * RING) + (holder // PLANE) * 2 + rank
 
 
 RING = 16
 PLANE = 8
 LANES = 4
 PART = 384
+HEAD = 128
+HEADS = 3
+CACHE = 768
 MESH = pl.DeviceIdType.MESH
 
 
@@ -90,19 +50,43 @@
     return jnp.dot(a, b, preferred_element_type=jnp.float32)
 
 
-def moe_kernel(
-    context_ref,
-    out_weight_ref,
+def dot_t(a, b):
+    return lax.dot_general(a, b, (((1,), (1,)), ((), ())), preferred_element_type=jnp.float32)
+
+
+def t_dot(a, b):
+    return lax.dot_general(a, b, (((0,), (0,)), ((), ())), preferred_element_type=jnp.float32)
+
+
+def layer_kernel(
     tokens_ref,
+    attn_gain_ref,
+    length_ref,
+    group_ref,
+    offset_ref,
+    sink_ref,
+    frequency_ref,
     mixer_ref,
-    places_ref,
-    places_t_ref,
+    routes_ref,
     route_weight_ref,
-    gate_ref,
-    up_ref,
-    down_ref,
+    copy_slot_ref,
     final_ref,
+    query_weight_hbm,
+    kv_weight_hbm,
+    cache_hbm,
+    out_weight_hbm,
+    gate_hbm,
+    up_hbm,
+    down_hbm,
     out_ref,
+    query_weight,
+    kv_weight,
+    cache,
+    out_weight,
+    gate,
+    up,
+    down,
+    new_kv,
     att,
     att_in,
     sq,
@@ -133,6 +117,9 @@
     r_sum,
     s_back,
     r_back,
+    s_kv,
+    r_kv,
+    s_load,
 ):
     me = lax.axis_index("expert")
     x = lax.axis_index("tensor")
@@ -158,10 +145,139 @@
     def _(d):
         greet(me, (x + d) % LANES)
 
-    context = context_ref[...]
+    half = x % 2
+    loads = [
+        pltpu.make_async_copy(src, dst, s_load.at[i])
+        for i, (src, dst) in enumerate(
+            [
+                (query_weight_hbm, query_weight),
+                (kv_weight_hbm, kv_weight),
+                (cache_hbm, cache.at[half]),
+                (out_weight_hbm, out_weight),
+                (gate_hbm, gate),
+                (up_hbm, up),
+                (down_hbm, down),
+            ]
+        )
+    ]
+    for load in loads:
+        load.start()
+
+    slots = 2 * RING * PLANE
+    copies = copy_slot_ref.shape[1]
+    replicas = copies // EXPERTS
+    group_rows = rows // replicas
+    early = lax.broadcasted_iota(jnp.int32, (rows, rows), 0)
+    late = lax.broadcasted_iota(jnp.int32, (rows, rows), 1)
+    before = (early // group_rows == late // group_rows) & (early < late)
+    before = before.astype(jnp.float32).astype(jnp.bfloat16)
+    expert_row = lax.broadcasted_iota(jnp.int32, (EXPERTS, rows), 0)
+    named = [
+        (routes_ref[k : k + 1, :] == expert_row).astype(jnp.float32) for k in range(TOP)
+    ]
+    earlier = dot(sum(named).astype(jnp.bfloat16), before)
+    copy_row = lax.broadcasted_iota(jnp.int32, (copies, rows), 0)
+    row_block = lax.broadcasted_iota(jnp.int32, (1, rows), 1) // group_rows
+    slot_of = jnp.broadcast_to(copy_slot_ref[...].astype(jnp.float32), (16, copies))
+    slot_of = slot_of.astype(jnp.bfloat16)
+    place_row = lax.broadcasted_iota(jnp.int32, (slots, rows), 0)
+    taken = jnp.zeros((slots, rows), jnp.float32)
+    weigh = jnp.zeros((slots, rows), jnp.float32)
+    for k in range(TOP):
+        rank = jnp.sum(named[k] * earlier, axis=0, keepdims=True).astype(jnp.int32)
+        wanted = routes_ref[k : k + 1, :] * replicas + row_block
+        picks = (wanted == copy_row).astype(jnp.float32).astype(jnp.bfloat16)
+        holder = dot(slot_of, picks)[:1].astype(jnp.int32)
+        place = (holder & (PLANE - 1)) * (2 * RING) + (holder >> 3) * 2 + rank
+        hit = place == place_row
+        taken = taken + hit.astype(jnp.float32)
+        weigh = weigh + jnp.where(hit, route_weight_ref[k : k + 1, :], 0.0)
+
+    values = tokens_ref[...].astype(jnp.float32)
+    normed_in = rms_scale(values, attn_gain_ref[...]).astype(jnp.bfloat16)
+
+    def column(row):
+        return jnp.sum(jnp.where(early == late, row.astype(jnp.float32), 0.0), axis=1, keepdims=True)
+
+    group = column(group_ref[...])
+    row_length = jnp.zeros((rows, 1), jnp.float32)
+    for p in range(length_ref.shape[1]):
+        this = length_ref[:, p : p + 1].astype(jnp.float32)
+        row_length = row_length + jnp.where(group == p, this, 0.0)
+    position = row_length + column(offset_ref[...])
+    angles = position * frequency_ref[...]
+    lane = lax.broadcasted_iota(jnp.int32, angles.shape, 1)
+    cosine = jnp.cos(angles)
+    sine = jnp.where(lane < HEAD // 2, -jnp.sin(angles), jnp.sin(angles))
+    loads[0].wait()
+    loads[1].wait()
+    queries = dot(normed_in, query_weight[...])
+    heads = []
+    for h in range(HEADS):
+        one = queries[:, h * HEAD : (h + 1) * HEAD]
+        heads.append(one * cosine + pltpu.roll(one, HEAD // 2, 1) * sine)
+    queries = jnp.concatenate(heads, axis=0).astype(jnp.bfloat16)
+    projected = dot(normed_in, kv_weight[...])
+    turned = projected * cosine + pltpu.roll(projected, HEAD // 2, 1) * sine
+    marks_key = lane * 0 + half == 0
+    new_kv[half] = jnp.where(marks_key, turned, projected).astype(jnp.bfloat16)
+    loads[2].wait()
+    pl.semaphore_wait(barrier, RING + PLANE + LANES - 3)
+
+    partner = x + 1 - 2 * half
+    new_copy = remote(
+        new_kv.at[half], new_kv.at[half], s_kv.at[0], r_kv.at[0], me, partner
+    )
+    cache_copy = remote(cache.at[half], cache.at[half], s_kv.at[1], r_kv.at[1], me, partner)
+    new_arrival = remote(
+        new_kv.at[half], new_kv.at[1 - half], s_kv.at[0], r_kv.at[0], me, partner
+    )
+    cache_arrival = remote(
+        cache.at[half], cache.at[1 - half], s_kv.at[1], r_kv.at[1], me, partner
+    )
+    new_copy.start()
+    cache_copy.start()
+
+    def stacked(block):
+        return jnp.concatenate([block] * HEADS, axis=0)
+
+    total_rows = HEADS * rows
+    scale = HEAD**-0.5
+    slot = lax.broadcasted_iota(jnp.int32, (rows, CACHE), 1)
+    slot_pos = (slot & (PROMPT_CAP - 1)).astype(jnp.float32)
+    visible = (
+        ((slot >> 8).astype(jnp.float32) == group)
+        & (slot_pos < row_length)
+        & (slot_pos > position - WINDOW)
+    )
+    visible = stacked(jnp.where(visible, 1.0, 0.0)) > 0.5
+    sinks = jnp.concatenate(
+        [jnp.broadcast_to(sink_ref[:, h : h + 1], (rows, 1)) for h in range(HEADS)], axis=0
+    )
+    new_arrival.wait_recv()
+    new_key = stacked(new_kv[0].astype(jnp.float32))
+    new_value = stacked(new_kv[1].astype(jnp.float32))
+    self_score = jnp.sum(queries.astype(jnp.float32) * new_key, axis=1, keepdims=True) * scale
+    cache_arrival.wait_recv()
+    scores = dot_t(queries, cache[0]) * scale
+    ceiling = jnp.max(jnp.where(visible, scores, -jnp.inf), axis=1, keepdims=True)
+    ceiling = jnp.maximum(jnp.maximum(ceiling, self_score), sinks)
+    weights = jnp.where(visible, jnp.exp(scores - ceiling), 0.0)
+    own_weight = jnp.exp(self_score - ceiling)
+    denominator = (
+        jnp.sum(weights, axis=1, keepdims=True) + own_weight + jnp.exp(sinks - ceiling)
+    )
+    probabilities = (weights / denominator).astype(jnp.bfloat16)
+    own_prob = (own_weight / denominator).astype(jnp.bfloat16).astype(jnp.float32)
+    context = dot(probabilities, cache[1]) + own_prob * new_value
+    context = context.astype(jnp.bfloat16)
+    context = jnp.concatenate(
+        [context[h * rows : (h + 1) * rows] for h in range(HEADS)], axis=1
+    )
+    loads[3].wait()
+
     for j in range(LANES):
-        att[j] = dot(context, out_weight_ref[:, j * PART : (j + 1) * PART]).astype(jnp.bfloat16)
-    pl.semaphore_wait(barrier, RING + PLANE + LANES - 3)
+        att[j] = dot(context, out_weight[:, j * PART : (j + 1) * PART]).astype(jnp.bfloat16)
 
     def att_copy(d):
         to = (x + d) % LANES
@@ -207,11 +323,6 @@
     gain = mixer_ref[:, mine].astype(jnp.float32)
     mixed = (residual * lax.rsqrt(total / width + EPSILON) * gain).astype(jnp.bfloat16)
 
-    slots = 2 * RING * PLANE
-    place_row = lax.broadcasted_iota(jnp.int32, (slots, rows), 0)
-    taken = jnp.zeros((slots, rows), jnp.float32)
-    for k in range(TOP):
-        taken = taken + (places_t_ref[k : k + 1, :] == place_row).astype(jnp.float32)
     outbox = dot(taken.astype(jnp.bfloat16), mixed).astype(jnp.bfloat16)
     plane_out[...] = outbox.reshape(PLANE, 2 * RING, PART)
 
@@ -308,15 +419,17 @@
         for j in range(1, LANES):
             box_arrival(d, j).wait_recv()
 
-    gate_val = jnp.zeros((slots, gate_ref.shape[1]), jnp.float32)
-    up_val = jnp.zeros((slots, gate_ref.shape[1]), jnp.float32)
+    for load in loads[4:]:
+        load.wait()
+    gate_val = jnp.zeros((slots, gate.shape[0]), jnp.float32)
+    up_val = jnp.zeros((slots, gate.shape[0]), jnp.float32)
     for j in range(LANES):
         part = box[j].reshape(slots, PART)
-        gate_val = gate_val + dot(part, gate_ref[j * PART : (j + 1) * PART, :])
-        up_val = up_val + dot(part, up_ref[j * PART : (j + 1) * PART, :])
+        gate_val = gate_val + dot_t(part, gate[:, j * PART : (j + 1) * PART])
+        up_val = up_val + dot_t(part, up[:, j * PART : (j + 1) * PART])
     hidden = (jnp.maximum(gate_val, 0.0) * up_val).astype(jnp.bfloat16)
     for j in range(LANES):
-        product = dot(hidden, down_ref[:, j * PART : (j + 1) * PART]).astype(jnp.bfloat16)
+        product = dot(hidden, down[:, j * PART : (j + 1) * PART]).astype(jnp.bfloat16)
         partial[j] = product.reshape(RING, 2 * PLANE, PART)
 
     def part_copy(d, j):
@@ -394,11 +507,6 @@
         back_copy(d).start()
 
     back_in[yc] = back_out[yc]
-    place_col = lax.broadcasted_iota(jnp.int32, (rows, slots), 1)
-    weigh = jnp.zeros((rows, slots), jnp.float32)
-    for k in range(TOP):
-        hit = places_ref[:, k : k + 1] == place_col
-        weigh = weigh + jnp.where(hit, route_weight_ref[:, k : k + 1], 0.0)
     high = weigh.astype(jnp.bfloat16)
     low = (weigh - high.astype(jnp.float32)).astype(jnp.bfloat16)
 
@@ -407,11 +515,13 @@
         back_arrival(d).wait_recv()
 
     returned = back_in[...].reshape(slots, PART)
-    combined = residual + (dot(high, returned) + dot(low, returned))
+    combined = residual + (t_dot(high, returned) + t_dot(low, returned))
     total = whole_square(combined, 1)
     final = final_ref[...].astype(jnp.float32)
     out_ref[...] = (combined * lax.rsqrt(total / width + EPSILON) * final).astype(out_ref.dtype)
 
+    new_copy.wait_send()
+    cache_copy.wait_send()
     for d in range(1, LANES):
         att_copy(d).wait_send()
 
@@ -432,18 +542,23 @@
             part_copy(d, j).wait_send()
 
 
-def moe_call(*operands):
-    rows = operands[2].shape[0]
+def layer_call(small, large):
+    rows = small[0].shape[0]
     vmem, sem = pltpu.VMEM, pltpu.SemaphoreType.DMA
     bf16 = jnp.bfloat16
     by_plane = vmem((PLANE, 2 * RING, PART), bf16)
     by_ring = vmem((RING, 2 * PLANE, PART), bf16)
+    held = [vmem(block.shape, bf16) for block in large]
+    held[2] = vmem((2, CACHE, HEAD), bf16)
     return pl.pallas_call(
-        moe_kernel,
+        layer_kernel,
         out_shape=jax.ShapeDtypeStruct((rows, PART), bf16),
-        in_specs=[pl.BlockSpec(memory_space=pltpu.VMEM)] * len(operands),
+        in_specs=[pl.BlockSpec(memory_space=pltpu.VMEM)] * len(small)
+        + [pl.BlockSpec(memory_space=pl.ANY)] * len(large),
         out_specs=pl.BlockSpec(memory_space=pltpu.VMEM),
-        scratch_shapes=[
+        scratch_shapes=held
+        + [
+            vmem((2, rows, HEAD), bf16),
             vmem((LANES, rows, PART), bf16),
             vmem((LANES - 1, rows, PART), bf16),
             vmem((2, rows, 128), jnp.float32),
@@ -465,9 +580,11 @@
         + [sem((RING,))] * 2
         + [sem((RING, LANES - 1))] * 4
         + [sem((RING,))] * 2
-        + [sem((PLANE,))] * 2,
+        + [sem((PLANE,))] * 2
+        + [sem((2,))] * 2
+        + [sem((7,))],
         compiler_params=pltpu.CompilerParams(collective_id=0, has_side_effects=True),
-    )(*operands)
+    )(*small, *large)
 
 
 def on_device(
@@ -490,82 +607,33 @@
     down_weight,
     final_gain,
 ):
-    lanes = lax.axis_size("tensor")
-    member = lax.axis_index("tensor")
-    peers = lax.axis_size("expert")
-    tok_rows, width = tokens.shape
-    head_dim = key_value_weight.shape[2]
-    local_heads = query_weight.shape[1] // head_dim
-    score_scale = 1.0 / head_dim**0.5
-    rows_f32 = tokens.astype(jnp.float32)
-    normed_in = rms_scale(rows_f32, attn_gain).astype(jnp.bfloat16)
-    lengths = prompt_length[0]
-    prompt_slots = jnp.arange(lengths.shape[0], dtype=jnp.int32)
-    row_length = jnp.sum(
-        jnp.where(group_index[:, None] == prompt_slots[None, :], lengths[None, :], 0), axis=1
-    )
-    position = row_length + offsets
-    queries = jnp.dot(normed_in, query_weight, preferred_element_type=jnp.float32).reshape(
-        tok_rows, local_heads, head_dim
-    )
-    queries = rotate(queries, position).astype(jnp.bfloat16)
-    projected = jnp.dot(normed_in, key_value_weight[0], preferred_element_type=jnp.float32)
-    marks_key = member % 2 == 0
-    own_projection = jnp.where(marks_key, rotate(projected, position), projected).astype(
-        jnp.bfloat16
-    )
-    own_cache = paired_cache[0, 0]
-    partner, partner_cache = from_partner((own_projection, own_cache), "tensor", 0)
-    new_keys = jnp.where(marks_key, own_projection, partner)
-    new_values = jnp.where(marks_key, partner, own_projection)
-    cache_keys = jnp.where(marks_key, own_cache, partner_cache)
-    cache_values = jnp.where(marks_key, partner_cache, own_cache)
-    scores = (
-        jnp.einsum("thd,cd->thc", queries, cache_keys, preferred_element_type=jnp.float32)
-        * score_scale
-    )
-    self_score = (
-        jnp.sum(queries.astype(jnp.float32) * new_keys.astype(jnp.float32)[:, None, :], axis=-1)
-        * score_scale
-    )
-    slot_index = jnp.arange(cache_keys.shape[0], dtype=jnp.int32)
-    slot_group = slot_index // PROMPT_CAP
-    slot_pos = slot_index % PROMPT_CAP
-    visible = (
-        (slot_group[None, :] == group_index[:, None])
-        & (slot_pos[None, :] < row_length[:, None])
-        & (slot_pos[None, :] > position[:, None] - WINDOW)
-    )
-    visible = visible[:, None, :]
-    masked = jnp.where(visible, scores, -jnp.inf)
-    ceiling = jnp.maximum(jnp.maximum(jnp.max(masked, axis=-1), self_score), sink_logit[None, :])
-    weights = jnp.where(visible, jnp.exp(scores - ceiling[..., None]), 0.0)
-    own_weight = jnp.exp(self_score - ceiling)
-    denominator = jnp.sum(weights, axis=-1) + own_weight + jnp.exp(sink_logit[None, :] - ceiling)
-    probabilities = (weights / denominator[..., None]).astype(jnp.bfloat16)
-    own_prob = (own_weight / denominator).astype(jnp.bfloat16)
-    context = jnp.einsum(
-        "thc,cd->thd", probabilities, cache_values, preferred_element_type=jnp.float32
-    )
-    context = (
-        context
-        + own_prob.astype(jnp.float32)[..., None] * new_values.astype(jnp.float32)[:, None, :]
-    )
-    context = context.astype(jnp.bfloat16).reshape(tok_rows, local_heads * head_dim)
-    places = slot_places(routes, copy_slot)
-    return moe_call(
-        context,
+    half = HEAD // 2
+    frequency = 10000.0 ** (-np.arange(half, dtype=np.float64) / half)
+    frequency = jnp.asarray(np.tile(frequency, 2)[None, :], jnp.float32)
+    small = [
+        tokens,
+        attn_gain.reshape(1, -1),
+        prompt_length,
+        group_index.reshape(1, -1),
+        offsets.reshape(1, -1),
+        sink_logit.reshape(1, -1),
+        frequency,
+        mixer_gain.reshape(1, -1),
+        routes.T,
+        route_weight.T,
+        copy_slot.reshape(1, -1),
+        final_gain.reshape(1, -1),
+    ]
+    large = [
+        query_weight,
+        key_value_weight[0],
+        paired_cache[0, 0],
         out_weight,
-        tokens,
-        mixer_gain.reshape(1, width),
-        places,
-        places.T,
-        route_weight,
-        gate_weight[0],
-        up_weight[0],
+        gate_weight[0].T,
+        up_weight[0].T,
         down_weight[0],
-        final_gain.reshape(1, -1),
-    )
+    ]
+    return layer_call(small, large)
 
 
 def solution(mesh):

time: 100 us -> 87.7 us (0.88)
  other arithmetic: 8.09 us -> 0 us
  Pallas kernels: 75.8 us -> 82.3 us
  starting transfers between devices: 5.85 us -> 0 us
  matrix products: 3.14 us -> 0 us
  local copies, waits for them, and re-layouts: 6.51 us -> 5.16 us
    pallas_call x1, Pallas kernels: 75.8 us -> 82.3 us  [layer_call(): pl.pallas_call(layer_kernel, out_shape=jax.ShapeDtypeStruct((rows, PART),...]
    ppermute x2 -> x0, starting transfers between devices: 5.85 us -> none  [from_partner(): return lax.ppermute(block, axis, route)]
    reduce_sum x6 -> x0, other arithmetic: 4.1 us -> none  [the longest x1 1.11 us: rms_scale(): mean_square = jnp.mean(values * values, axis=-1, keepdims=True)]
    dot_general x4 -> x0, matrix products: 3.14 us -> none  [the longest x1 1.29 us: on_device(): jnp.dot(normed_in, key_value_weight[0], preferred_element_type=jnp.float32)]
    unnamed x22 -> x1, local copies, waits for them, and re-layouts: 4.41 us -> 1.35 us
    add x3 -> x0, other arithmetic: 1.92 us -> none  [the longest x2 1.23 us: slot_places(): return holder % PLANE * (2 * RING) + holder // PLANE * 2 + rank]
    reshape x3 -> x2, local copies, waits for them, and re-layouts: 1.23 us -> 2.56 us  [the longest x1 1.28 us: on_device(): attn_gain.reshape(1, -1)]
  transfers between devices with their start and end apart: 2 -> 0, of which waited for: 0 -> 0; matrix products, arithmetic and copies ran while one was open for 10% -> 0% of each run, Pallas kernels for 0% -> 0%
where the time goes in v3:
time: 87.7 us; the launch traced here: 87.5 us
  Pallas kernels  82.3 us (94%)
  local copies, waits for them, and re-layouts  5.16 us (6%)
    pallas_call x1, Pallas kernels, layer_call(): pl.pallas_call(layer_kernel, out_shape=jax.ShapeDtypeStruct((rows, PART),...  82.3 us

profile of v3, /device:TPU:1, one launch (start us, length us, event | category | flops | bytes accessed | tf_op | source)
XLA Modules:
  0.0 87.5 jit_solution(12037072815085288231)
XLA Ops:
  0.0 1.3 %reshape.27.final_ref = bf16[1,384]{1,0:T(2,128)(2,1)} reshape(bf16[384]{0:T(512)(128)(2,1)} %param.36) | data formatting | bytes 1536 | tf_op jit(solution)/shard_map/reshape | solution.py:625
  1.3 1.3 %reshape.21.attn_gain_ref = bf16[1,1536]{1,0:T(2,128)(2,1)} reshape(bf16[1536]{0:T(1024)(128)(2,1)} %param.20) | data formatting | bytes 6144 | tf_op jit(solution)/shard_map/reshape | solution.py:615
  2.5 1.3 %reshape.25.mixer_ref = bf16[1,1536]{1,0:T(2,128)(2,1)} reshape(bf16[1536]{0:T(1024)(128)(2,1)} %param.29) | data formatting | bytes 6144 | tf_op jit(solution)/shard_map/reshape | solution.py:621
  3.8 82.3 %shard_map.181 = bf16[32,384]{1,0:T(8,128)(2,1)} custom-call(bf16[32,1536]{1,0:T(8,128)(2,1)} %tokens_ref.1, bf16[1,1536]{1,0:T(2,128)(2,1)} %reshape.21.attn_gain_ref, s32[1,3]{1,0:T(1,128)} %length_ref.1, s32[1,32]{1,0:T(1,128)} %bitcast.22, s32[1,32]{1,0:T(1,128)} %bitcast.23, f32[1,3]{1,0:T(1,128)} %bitcast.24, f32[1,128]{1,0:T(1,128)} %constant.2.clone.frequency_ref, ...), custom_call_target="tpu_custom_call" | custom-call | tf_op jit(solution)/shard_map/pallas_call | solution.py:553
  86.1 1.3 %copy.21 = bf16[32,384]{1,0:T(8,128)(2,1)} copy(bf16[32,384]{1,0:T(8,128)(2,1)} %shard_map.181) | data formatting | bytes 49152

commit v4 on v3

--- a/solution.py
+++ b/solution.py
@@ -52,6 +52,10 @@
 
 def dot_t(a, b):
     return lax.dot_general(a, b, (((1,), (1,)), ((), ())), preferred_element_type=jnp.float32)
+
+
+def as_row(values):
+    return values.astype(jnp.float32).reshape(1, -1)
 
 
 def t_dot(a, b):
@@ -194,7 +198,7 @@
         weigh = weigh + jnp.where(hit, route_weight_ref[k : k + 1, :], 0.0)
 
     values = tokens_ref[...].astype(jnp.float32)
-    normed_in = rms_scale(values, attn_gain_ref[...]).astype(jnp.bfloat16)
+    normed_in = rms_scale(values, as_row(attn_gain_ref[...])).astype(jnp.bfloat16)
 
     def column(row):
         return jnp.sum(jnp.where(early == late, row.astype(jnp.float32), 0.0), axis=1, keepdims=True)
@@ -320,7 +324,11 @@
         return total
 
     total = whole_square(residual, 0)
-    gain = mixer_ref[:, mine].astype(jnp.float32)
+    gains = as_row(mixer_ref[...])
+    gain = jnp.zeros((1, PART), jnp.float32)
+    for j in range(LANES):
+        this = (x == j).astype(jnp.float32)
+        gain = gain + this * gains[:, j * PART : (j + 1) * PART]
     mixed = (residual * lax.rsqrt(total / width + EPSILON) * gain).astype(jnp.bfloat16)
 
     outbox = dot(taken.astype(jnp.bfloat16), mixed).astype(jnp.bfloat16)
@@ -517,7 +525,7 @@
     returned = back_in[...].reshape(slots, PART)
     combined = residual + (t_dot(high, returned) + t_dot(low, returned))
     total = whole_square(combined, 1)
-    final = final_ref[...].astype(jnp.float32)
+    final = as_row(final_ref[...]).astype(jnp.float32)
     out_ref[...] = (combined * lax.rsqrt(total / width + EPSILON) * final).astype(out_ref.dtype)
 
     new_copy.wait_send()
@@ -612,17 +620,17 @@
     frequency = jnp.asarray(np.tile(frequency, 2)[None, :], jnp.float32)
     small = [
         tokens,
-        attn_gain.reshape(1, -1),
+        attn_gain,
         prompt_length,
         group_index.reshape(1, -1),
         offsets.reshape(1, -1),
         sink_logit.reshape(1, -1),
         frequency,
-        mixer_gain.reshape(1, -1),
+        mixer_gain,
         routes.T,
         route_weight.T,
         copy_slot.reshape(1, -1),
-        final_gain.reshape(1, -1),
+        final_gain,
     ]
     large = [
         query_weight,

time: 87.7 us -> 83.6 us (0.953)
  local copies, waits for them, and re-layouts: 5.16 us -> 1.35 us
    reshape x3 -> x0, local copies, waits for them, and re-layouts: 3.82 us -> none  [the longest x1 1.28 us: on_device(): attn_gain.reshape(1, -1)]
where the time goes in v4:
time: 83.6 us; the launch traced here: 83.4 us
  Pallas kernels  82 us (98%)
  local copies, waits for them, and re-layouts  1.35 us (2%)
    pallas_call x1, Pallas kernels, layer_call(): pl.pallas_call(layer_kernel, out_shape=jax.ShapeDtypeStruct((rows, PART),...  82 us

profile of v4, /device:TPU:1, one launch (start us, length us, event | category | flops | bytes accessed | tf_op | source)
XLA Modules:
  0.0 83.4 jit_solution(9583010762720748265)
XLA Ops:
  0.0 82.0 %shard_map.181 = bf16[32,384]{1,0:T(8,128)(2,1)} custom-call(bf16[32,1536]{1,0:T(8,128)(2,1)} %tokens_ref.1, bf16[1536]{0:T(1024)(128)(2,1)} %attn_gain_ref.1, s32[1,3]{1,0:T(1,128)} %length_ref.1, s32[1,32]{1,0:T(1,128)} %bitcast.22, s32[1,32]{1,0:T(1,128)} %bitcast.23, f32[1,3]{1,0:T(1,128)} %bitcast.24, f32[1,128]{1,0:T(1,128)} %constant.2.clone.frequency_ref, ...), custom_call_target="tpu_custom_call" | custom-call | tf_op jit(solution)/shard_map/pallas_call | solution.py:561
  82.0 1.3 %copy.21 = bf16[32,384]{1,0:T(8,128)(2,1)} copy(bf16[32,384]{1,0:T(8,128)(2,1)} %shard_map.181) | data formatting | bytes 49152

commit v5 on v4

--- a/solution.py
+++ b/solution.py
@@ -213,6 +213,11 @@
     lane = lax.broadcasted_iota(jnp.int32, angles.shape, 1)
     cosine = jnp.cos(angles)
     sine = jnp.where(lane < HEAD // 2, -jnp.sin(angles), jnp.sin(angles))
+    loads[2].wait()
+    pl.semaphore_wait(barrier, RING + PLANE + LANES - 3)
+    partner = x + 1 - 2 * half
+    cache_copy = remote(cache.at[half], cache.at[half], s_kv.at[1], r_kv.at[1], me, partner)
+    cache_copy.start()
     loads[0].wait()
     loads[1].wait()
     queries = dot(normed_in, query_weight[...])
@@ -225,14 +230,9 @@
     turned = projected * cosine + pltpu.roll(projected, HEAD // 2, 1) * sine
     marks_key = lane * 0 + half == 0
     new_kv[half] = jnp.where(marks_key, turned, projected).astype(jnp.bfloat16)
-    loads[2].wait()
-    pl.semaphore_wait(barrier, RING + PLANE + LANES - 3)
-
-    partner = x + 1 - 2 * half
     new_copy = remote(
         new_kv.at[half], new_kv.at[half], s_kv.at[0], r_kv.at[0], me, partner
     )
-    cache_copy = remote(cache.at[half], cache.at[half], s_kv.at[1], r_kv.at[1], me, partner)
     new_arrival = remote(
         new_kv.at[half], new_kv.at[1 - half], s_kv.at[0], r_kv.at[0], me, partner
     )
@@ -240,7 +240,6 @@
         cache.at[half], cache.at[1 - half], s_kv.at[1], r_kv.at[1], me, partner
     )
     new_copy.start()
-    cache_copy.start()
 
     def stacked(block):
         return jnp.concatenate([block] * HEADS, axis=0)

time: 83.6 us -> 83.8 us (level)
  no operation moved by 1% of the time
where the time goes in v5:
time: 83.8 us; the launch traced here: 83.6 us
  Pallas kernels  82.2 us (98%)
  local copies, waits for them, and re-layouts  1.35 us (2%)
    pallas_call x1, Pallas kernels, layer_call(): pl.pallas_call(layer_kernel, out_shape=jax.ShapeDtypeStruct((rows, PART),...  82.2 us

profile of v5, /device:TPU:1, one launch (start us, length us, event | category | flops | bytes accessed | tf_op | source)
XLA Modules:
  0.0 83.6 jit_solution(5396712538138181597)
XLA Ops:
  0.0 82.2 %shard_map.181 = bf16[32,384]{1,0:T(8,128)(2,1)} custom-call(bf16[32,1536]{1,0:T(8,128)(2,1)} %tokens_ref.1, bf16[1536]{0:T(1024)(128)(2,1)} %attn_gain_ref.1, s32[1,3]{1,0:T(1,128)} %length_ref.1, s32[1,32]{1,0:T(1,128)} %bitcast.22, s32[1,32]{1,0:T(1,128)} %bitcast.23, f32[1,3]{1,0:T(1,128)} %bitcast.24, f32[1,128]{1,0:T(1,128)} %constant.2.clone.frequency_ref, ...), custom_call_target="tpu_custom_call" | custom-call | tf_op jit(solution)/shard_map/pallas_call | solution.py:560
  82.2 1.3 %copy.21 = bf16[32,384]{1,0:T(8,128)(2,1)} copy(bf16[32,384]{1,0:T(8,128)(2,1)} %shard_map.181) | data formatting | bytes 49152
